TPU v7x, 32 devices: a whole 2x2x4 slice. The times are simulated.
32 devices in a mesh: loan: 8 (over y, x, core), path: 4 (over z).
Axes of the slice: x: 2, y: 2, z: 4, core: 2. Of those that a mesh axis runs over, the one named last changes fastest.
Arguments:
- price_moves: bfloat16 [12, 416, 512], P(None, 'loan', 'path'), may hold values from -0.1796875 to 0.1796875
- block_regions: int32 [16, 32], P('loan'), may hold values from 0 to 415
- region_slot: int32 [4096], P('loan'), may hold values from 0 to 31
- block_pools: int32 [16, 32], P('loan'), may hold values from 0 to 511, as said below
- pool_slot: int32 [4096], P('loan'), may hold values from 0 to 31, as said below
- init_state: int32 [4096], P('loan'), may hold values from 0 to 5
- balance: float32 [4096], P('loan'), may hold values from 0.5 to 2
- loan_to_value: float32 [4096], P('loan'), may hold values from 0.5 to 1.3
- hazard_base: float32 [2, 6], replicated, may hold values from -4 to -1
- hazard_slope: float32 [2, 6], replicated, may hold values from 1 to 4
- attach_bps: int32 [512, 6], P('loan'), may hold values from 0 to 2995, as said below
Outputs:
- expected_loss: float32 [6, 3, 512], P(None, None, 'loan')
- path_loss: float32 [6, 512, 512], P(None, 'loan', 'path')
Inputs may be any that keep to these rules, and one draw needn't show every extreme that they name: `block_pools`: over all blocks' lists every pool appears exactly once. The lists of the blocks held by one index of loan name exactly 64 // 8 pools of every owner, owner k being the index of loan that holds pools k * 64 to (k + 1) * 64 - 1. `pool_slot`: every aligned block of 256 loans uses each position of its pool list at least once. `attach_bps`: each row starts at 0 and rises by 100 to 599 from one tranche to the next.
All inputs are finite; a program needn't handle non-finite values.
Results may differ from a plain program's by a relative error of at most 0.0003.
Values may be sent and summed in bfloat16 or wider, within the bound.
No kernel may reach another device: no remote copies, remote signals or barrier semaphores. Data moves between devices by JAX's collectives and lax.ppermute only.
A program may use at most 64 MiB of HBM per device.

v0:
```python
import jax
import jax.numpy as jnp
from jax import lax
from jax.sharding import PartitionSpec as P

BLOCK = 256


stress_scale = 0.3


def roll_months(
    routed, path_place, path_count, log_value, initial, balance, hazard_base, hazard_slope
):
    months = routed.shape[0]
    month_place = (jnp.arange(months, dtype=jnp.float32) + 1.0) / months
    stress_path = (
        stress_scale * ((path_place + 0.5) / path_count)[None, :, None] * month_place[:, None, None]
    )
    cumulated = jnp.cumsum(routed, axis=0) - stress_path
    level = log_value[None, None, :] - cumulated
    start_state = jnp.broadcast_to(
        initial[:, None, :], (initial.shape[0], routed.shape[1], routed.shape[2])
    )
    loss_start = jnp.zeros(routed.shape[1:], jnp.float32)

    def month_step(state_pair, ltv_now):
        state, loss_sum = state_pair
        roll_rate = jax.nn.sigmoid(
            hazard_base[0][:, None, None] + hazard_slope[0][:, None, None] * ltv_now[None]
        )
        cure_rate = jax.nn.sigmoid(
            hazard_base[1][:, None, None] - hazard_slope[1][:, None, None] * ltv_now[None]
        )
        stay_rate = (1.0 - roll_rate) * (1.0 - cure_rate)
        forward = state * roll_rate
        backward = state * (1.0 - roll_rate) * cure_rate
        first_state = state[0] * stay_rate[0] + jnp.sum(backward[1:], axis=0)
        rest_state = forward[:-1] + state[1:] * stay_rate[1:]
        updated = jnp.concatenate([first_state[None], rest_state], axis=0)
        severity = 0.1 + 0.5 * jax.nn.sigmoid(3.0 * ltv_now)
        loss_next = loss_sum + balance[None, :] * severity * forward[-1]
        return ((updated, loss_next), loss_next)

    state_pair, history = lax.scan(month_step, (start_state, loss_start), level)
    return history[3::4]


def lookup(lookup_table, positions):
    matches = positions[:, None] == jnp.arange(lookup_table.shape[0], dtype=jnp.int32)[None, :]
    return jnp.sum(jnp.where(matches, lookup_table[None, :], 0), axis=1)


def shards(
    price_moves,
    block_regions,
    region_slot,
    block_pools,
    pool_slot,
    init_state,
    balance,
    loan_to_value,
    hazard_base,
    hazard_slope,
    attach_bps,
):
    loan_dev = region_slot.shape[0]
    months, metro_dev, path_dev = price_moves.shape
    pool_dev = attach_bps.shape[0]
    dates = months // 4
    block_index = jnp.arange(loan_dev, dtype=jnp.int32) // BLOCK
    metro_id = lookup(block_regions.reshape(-1), block_index * block_regions.shape[1] + region_slot)
    slot_id = block_index * block_pools.shape[1] + pool_slot
    listed_pools = block_pools.reshape(-1)
    shard = lax.all_gather(price_moves, "loan", axis=1, tiled=True)
    chooser = (metro_id[None, :] == jnp.arange(shard.shape[1], dtype=jnp.int32)[:, None]).astype(
        jnp.bfloat16
    )
    routed = jnp.einsum("mrp,rl->mpl", shard, chooser, preferred_element_type=jnp.float32)
    path_count = path_dev * lax.axis_size("path")
    path_place = (lax.axis_index("path") * path_dev + jnp.arange(path_dev, dtype=jnp.int32)).astype(
        jnp.float32
    )
    initial = (
        init_state[None, :] == jnp.arange(hazard_base.shape[1], dtype=jnp.int32)[:, None]
    ).astype(jnp.float32)
    losses = roll_months(
        routed,
        path_place,
        float(path_count),
        jnp.log(loan_to_value),
        initial,
        balance,
        hazard_base,
        hazard_slope,
    )
    loss_rows = losses.reshape(dates * path_dev, loan_dev)
    contract = (((1,), (1,)), ((), ()))
    slot_count = listed_pools.shape[0]
    members = (slot_id[None, :] == jnp.arange(slot_count, dtype=jnp.int32)[:, None]).astype(
        jnp.float32
    )
    slot_loss = lax.dot_general(
        members,
        loss_rows,
        contract,
        precision=lax.Precision.HIGHEST,
        preferred_element_type=jnp.float32,
    )
    slot_balance = jnp.dot(
        members, balance, precision=lax.Precision.HIGHEST, preferred_element_type=jnp.float32
    )
    ranking = jnp.argsort(listed_pools // pool_dev, stable=True)
    outgoing = (
        slot_loss[ranking],
        slot_balance[ranking],
        listed_pools[ranking].astype(jnp.float32),
    )
    got_loss, got_balance, got_pool = (
        lax.all_to_all(outgoing[0], "loan", split_axis=0, concat_axis=0, tiled=True),
        lax.all_to_all(outgoing[1], "loan", split_axis=0, concat_axis=0, tiled=True),
        lax.all_to_all(outgoing[2], "loan", split_axis=0, concat_axis=0, tiled=True),
    )
    local_pool = got_pool - (lax.axis_index("loan") * pool_dev).astype(jnp.float32)
    placing = (
        local_pool[None, :] == jnp.arange(pool_dev, dtype=jnp.int32)[:, None].astype(jnp.float32)
    ).astype(jnp.float32)
    pool_loss = jnp.dot(
        placing, got_loss, precision=lax.Precision.HIGHEST, preferred_element_type=jnp.float32
    )
    notional = jnp.dot(
        placing, got_balance, precision=lax.Precision.HIGHEST, preferred_element_type=jnp.float32
    )
    attach = attach_bps.astype(jnp.float32) / 10000.0
    detach = jnp.concatenate([attach[:, 1:], jnp.ones((pool_dev, 1), jnp.float32)], axis=1)
    ratio = pool_loss.reshape(pool_dev, dates, path_dev) / notional[:, None, None]
    lower = attach.T[:, :, None, None]
    height = (detach - attach).T[:, :, None, None]
    shares = jnp.clip((ratio[None] - lower) / height, 0.0, 1.0)
    partial_value = jnp.sum(shares, axis=3).transpose(0, 2, 1)
    expected_loss = lax.psum(partial_value, "path") / path_count
    return (expected_loss, shares[:, :, -1, :])


def solution(mesh):
    in_specs = (
        P(None, "loan", "path"),
        P("loan", None),
        P("loan"),
        P("loan", None),
        P("loan"),
        P("loan"),
        P("loan"),
        P("loan"),
        P(),
        P(),
        P("loan", None),
    )
    out_specs = (P(None, None, "loan"), P(None, "loan", "path"))
    return jax.shard_map(shards, mesh=mesh, in_specs=in_specs, out_specs=out_specs, check_vma=False)
```

profile of v0, /device:TPU:0, one launch (start us, length us, event | category | flops | bytes accessed | tf_op | source)
XLA Modules:
  0.0 173.0 jit_solution(12231268295599842908)
XLA Ops:
  13.2 5.2 %all-to-all-start = ((f32[8,8,1]{1,2,0:T(1,128)}), f32[8,8,1]{1,2,0:T(1,128)S(1)}, u32[]{:S(2)}, u32[]{:S(2)}) async-start(f32[8,8,1]{1,2,0:T(1,128)} %bitcast), calls=%async_computation | async-start | bytes 8192 | tf_op jit(solution)/shard_map/all_to_all | solution.py:122
  23.0 3.3 %all-to-all-start.2 = ((f32[8,8,1]{1,2,0:T(1,128)}), f32[8,8,1]{1,2,0:T(1,128)S(1)}, u32[]{:S(2)}, u32[]{:S(2)}) async-start(f32[8,8,1]{1,2,0:T(1,128)} %bitcast.10), calls=%async_computation.2 | async-start | bytes 8192 | tf_op jit(solution)/shard_map/all_to_all | solution.py:121
  26.5 4.4 %all-to-all-done.2 = f32[8,8,1]{1,2,0:T(1,128)S(1)} async-done(((f32[8,8,1]{1,2,0:T(1,128)}), f32[8,8,1]{1,2,0:T(1,128)S(1)}, u32[]{:S(2)}, u32[]{:S(2)}) %all-to-all-start.2) | async-done | bytes 288 | tf_op jit(solution)/shard_map/all_to_all | solution.py:121
  32.2 6.6 %all-gather.2.cloned.1.call-done = bf16[12,416,128]{2,0,1:T(8,128)(2,1)} async-done(((bf16[12,52,128]{2,0,1:T(8,128)(2,1)}), bf16[12,416,128]{2,0,1:T(8,128)(2,1)}) %all-gather.2.cloned.1.call-update) | async-done | bytes 1277968 | tf_op jit(solution)/shard_map/all_gather | solution.py:75
  38.8 2.5 %fusion.9 = f32[512,12,128]{2,0,1:T(8,128)S(1)} fusion(bf16[12,416,128]{2,0,1:T(8,128)(2,1)} %all-gather.2.cloned.1.call-done, s32[512]{0:T(512)S(1)} %select_reduce_fusion), kind=kOutput, calls=%fused_computation.28 | convolution fusion | flops 654524416 | bytes 4425728 | tf_op jit(solution)/shard_map/mrp,rl->mpl/dot_general | solution.py:79
  44.1 89.9 %while.15 = (s32[]{:T(128)}, f32[6,128,512]{2,1,0:T(8,128)S(1)}, f32[128,512]{1,0:T(8,128)}, f32[12,128,512]{2,1,0:T(8,128)}, f32[2,6]{1,0:T(2,128)S(1)}, /*inde...) while((s32[]{:T(128)}, f32[6,128,512]{2,1,0:T(8,128)S(1)}, ...), condition=%wide.region_5.6_spmd.clone, body=%wide.region_3.5_spmd.clone.sunk | while | flops 8257539 | bytes 34343880 | solution.py:45
  46.4 2.7 %fusion.43 = (f32[128,512]{1,0:T(8,128)}, f32[5,128,512]{2,1,0:T(8,128)}) fusion(f32[6,128,512]{2,1,0:T(8,128)S(1)} %get-tuple-element.209, f32[6,128,512]{2,1,0:T(8,128)S(1)} %get-tuple-element.210, f32[6,128,512]{2,1,0:T(8,128)S(1)} %get-tuple-element.229, f32[6,128,512]{2,1,0:T(8,128)S(1)} %get-tuple-element.211, ...), kind=kLoop, calls=%fused_computation.10.clone.1 | loop fusion | flops 1572864 | bytes 8126464 | tf_op jit(solution)/shard_map/while/body/eval_jaxpr/reduce_sum | solution.py:38
  53.9 2.7 %fusion.43 = (f32[128,512]{1,0:T(8,128)}, f32[5,128,512]{2,1,0:T(8,128)}) fusion(f32[6,128,512]{2,1,0:T(8,128)S(1)} %get-tuple-element.209, f32[6,128,512]{2,1,0:T(8,128)S(1)} %get-tuple-element.210, f32[6,128,512]{2,1,0:T(8,128)S(1)} %get-tuple-element.229, f32[6,128,512]{2,1,0:T(8,128)S(1)} %get-tuple-element.211, ...), kind=kLoop, calls=%fused_computation.10.clone.1 | loop fusion | flops 1572864 | bytes 8126464 | tf_op jit(solution)/shard_map/while/body/eval_jaxpr/reduce_sum | solution.py:38
  56.6 2.2 %bitcast_dynamic-update-slice_fusion.2 = (f32[12,128,512]{2,1,0:T(8,128)}, f32[128,512]{1,0:T(8,128)}, f32[1,128,512]{2,1,0:T(8,128)S(1)}) fusion(f32[12,128,512]{2,1,0:T(8,128)} %get-tuple-element.231, s32[]{:T(128)} %get-tuple-element.228, f32[6,128,512]{2,1,0:T(8,128)S(1)} %get-tuple-element.212, f32[1,128,512]{2,1,0:T(8,128)S(1)} %copy.39, ...), kind=kLoop, calls=%fused_computation.19.clone.1 | loop fusion | flops 786432 | bytes 2361857 | tf_op jit(solution)/shard_map/while/body/jit(dynamic_update_index_in_dim)/dynamic_update_slice | solution.py:45
  61.4 2.7 %fusion.43 = (f32[128,512]{1,0:T(8,128)}, f32[5,128,512]{2,1,0:T(8,128)}) fusion(f32[6,128,512]{2,1,0:T(8,128)S(1)} %get-tuple-element.209, f32[6,128,512]{2,1,0:T(8,128)S(1)} %get-tuple-element.210, f32[6,128,512]{2,1,0:T(8,128)S(1)} %get-tuple-element.229, f32[6,128,512]{2,1,0:T(8,128)S(1)} %get-tuple-element.211, ...), kind=kLoop, calls=%fused_computation.10.clone.1 | loop fusion | flops 1572864 | bytes 8126464 | tf_op jit(solution)/shard_map/while/body/eval_jaxpr/reduce_sum | solution.py:38
  64.1 2.2 %bitcast_dynamic-update-slice_fusion.2 = (f32[12,128,512]{2,1,0:T(8,128)}, f32[128,512]{1,0:T(8,128)}, f32[1,128,512]{2,1,0:T(8,128)S(1)}) fusion(f32[12,128,512]{2,1,0:T(8,128)} %get-tuple-element.231, s32[]{:T(128)} %get-tuple-element.228, f32[6,128,512]{2,1,0:T(8,128)S(1)} %get-tuple-element.212, f32[1,128,512]{2,1,0:T(8,128)S(1)} %copy.39, ...), kind=kLoop, calls=%fused_computation.19.clone.1 | loop fusion | flops 786432 | bytes 2361857 | tf_op jit(solution)/shard_map/while/body/jit(dynamic_update_index_in_dim)/dynamic_update_slice | solution.py:45
  68.9 2.7 %fusion.43 = (f32[128,512]{1,0:T(8,128)}, f32[5,128,512]{2,1,0:T(8,128)}) fusion(f32[6,128,512]{2,1,0:T(8,128)S(1)} %get-tuple-element.209, f32[6,128,512]{2,1,0:T(8,128)S(1)} %get-tuple-element.210, f32[6,128,512]{2,1,0:T(8,128)S(1)} %get-tuple-element.229, f32[6,128,512]{2,1,0:T(8,128)S(1)} %get-tuple-element.211, ...), kind=kLoop, calls=%fused_computation.10.clone.1 | loop fusion | flops 1572864 | bytes 8126464 | tf_op jit(solution)/shard_map/while/body/eval_jaxpr/reduce_sum | solution.py:38
  76.4 2.7 %fusion.43 = (f32[128,512]{1,0:T(8,128)}, f32[5,128,512]{2,1,0:T(8,128)}) fusion(f32[6,128,512]{2,1,0:T(8,128)S(1)} %get-tuple-element.209, f32[6,128,512]{2,1,0:T(8,128)S(1)} %get-tuple-element.210, f32[6,128,512]{2,1,0:T(8,128)S(1)} %get-tuple-element.229, f32[6,128,512]{2,1,0:T(8,128)S(1)} %get-tuple-element.211, ...), kind=kLoop, calls=%fused_computation.10.clone.1 | loop fusion | flops 1572864 | bytes 8126464 | tf_op jit(solution)/shard_map/while/body/eval_jaxpr/reduce_sum | solution.py:38
  83.9 2.7 %fusion.43 = (f32[128,512]{1,0:T(8,128)}, f32[5,128,512]{2,1,0:T(8,128)}) fusion(f32[6,128,512]{2,1,0:T(8,128)S(1)} %get-tuple-element.209, f32[6,128,512]{2,1,0:T(8,128)S(1)} %get-tuple-element.210, f32[6,128,512]{2,1,0:T(8,128)S(1)} %get-tuple-element.229, f32[6,128,512]{2,1,0:T(8,128)S(1)} %get-tuple-element.211, ...), kind=kLoop, calls=%fused_computation.10.clone.1 | loop fusion | flops 1572864 | bytes 8126464 | tf_op jit(solution)/shard_map/while/body/eval_jaxpr/reduce_sum | solution.py:38
  91.4 2.7 %fusion.43 = (f32[128,512]{1,0:T(8,128)}, f32[5,128,512]{2,1,0:T(8,128)}) fusion(f32[6,128,512]{2,1,0:T(8,128)S(1)} %get-tuple-element.209, f32[6,128,512]{2,1,0:T(8,128)S(1)} %get-tuple-element.210, f32[6,128,512]{2,1,0:T(8,128)S(1)} %get-tuple-element.229, f32[6,128,512]{2,1,0:T(8,128)S(1)} %get-tuple-element.211, ...), kind=kLoop, calls=%fused_computation.10.clone.1 | loop fusion | flops 1572864 | bytes 8126464 | tf_op jit(solution)/shard_map/while/body/eval_jaxpr/reduce_sum | solution.py:38
  98.9 2.7 %fusion.43 = (f32[128,512]{1,0:T(8,128)}, f32[5,128,512]{2,1,0:T(8,128)}) fusion(f32[6,128,512]{2,1,0:T(8,128)S(1)} %get-tuple-element.209, f32[6,128,512]{2,1,0:T(8,128)S(1)} %get-tuple-element.210, f32[6,128,512]{2,1,0:T(8,128)S(1)} %get-tuple-element.229, f32[6,128,512]{2,1,0:T(8,128)S(1)} %get-tuple-element.211, ...), kind=kLoop, calls=%fused_computation.10.clone.1 | loop fusion | flops 1572864 | bytes 8126464 | tf_op jit(solution)/shard_map/while/body/eval_jaxpr/reduce_sum | solution.py:38
  101.6 2.3 %bitcast_dynamic-update-slice_fusion.2 = (f32[12,128,512]{2,1,0:T(8,128)}, f32[128,512]{1,0:T(8,128)}, f32[1,128,512]{2,1,0:T(8,128)S(1)}) fusion(f32[12,128,512]{2,1,0:T(8,128)} %get-tuple-element.231, s32[]{:T(128)} %get-tuple-element.228, f32[6,128,512]{2,1,0:T(8,128)S(1)} %get-tuple-element.212, f32[1,128,512]{2,1,0:T(8,128)S(1)} %copy.39, ...), kind=kLoop, calls=%fused_computation.19.clone.1 | loop fusion | flops 786432 | bytes 2361857 | tf_op jit(solution)/shard_map/while/body/jit(dynamic_update_index_in_dim)/dynamic_update_slice | solution.py:45
  106.4 2.7 %fusion.43 = (f32[128,512]{1,0:T(8,128)}, f32[5,128,512]{2,1,0:T(8,128)}) fusion(f32[6,128,512]{2,1,0:T(8,128)S(1)} %get-tuple-element.209, f32[6,128,512]{2,1,0:T(8,128)S(1)} %get-tuple-element.210, f32[6,128,512]{2,1,0:T(8,128)S(1)} %get-tuple-element.229, f32[6,128,512]{2,1,0:T(8,128)S(1)} %get-tuple-element.211, ...), kind=kLoop, calls=%fused_computation.10.clone.1 | loop fusion | flops 1572864 | bytes 8126464 | tf_op jit(solution)/shard_map/while/body/eval_jaxpr/reduce_sum | solution.py:38
  113.9 2.7 %fusion.43 = (f32[128,512]{1,0:T(8,128)}, f32[5,128,512]{2,1,0:T(8,128)}) fusion(f32[6,128,512]{2,1,0:T(8,128)S(1)} %get-tuple-element.209, f32[6,128,512]{2,1,0:T(8,128)S(1)} %get-tuple-element.210, f32[6,128,512]{2,1,0:T(8,128)S(1)} %get-tuple-element.229, f32[6,128,512]{2,1,0:T(8,128)S(1)} %get-tuple-element.211, ...), kind=kLoop, calls=%fused_computation.10.clone.1 | loop fusion | flops 1572864 | bytes 8126464 | tf_op jit(solution)/shard_map/while/body/eval_jaxpr/reduce_sum | solution.py:38
  121.4 2.7 %fusion.43 = (f32[128,512]{1,0:T(8,128)}, f32[5,128,512]{2,1,0:T(8,128)}) fusion(f32[6,128,512]{2,1,0:T(8,128)S(1)} %get-tuple-element.209, f32[6,128,512]{2,1,0:T(8,128)S(1)} %get-tuple-element.210, f32[6,128,512]{2,1,0:T(8,128)S(1)} %get-tuple-element.229, f32[6,128,512]{2,1,0:T(8,128)S(1)} %get-tuple-element.211, ...), kind=kLoop, calls=%fused_computation.10.clone.1 | loop fusion | flops 1572864 | bytes 8126464 | tf_op jit(solution)/shard_map/while/body/eval_jaxpr/reduce_sum | solution.py:38
  128.9 2.7 %fusion.43 = (f32[128,512]{1,0:T(8,128)}, f32[5,128,512]{2,1,0:T(8,128)}) fusion(f32[6,128,512]{2,1,0:T(8,128)S(1)} %get-tuple-element.209, f32[6,128,512]{2,1,0:T(8,128)S(1)} %get-tuple-element.210, f32[6,128,512]{2,1,0:T(8,128)S(1)} %get-tuple-element.229, f32[6,128,512]{2,1,0:T(8,128)S(1)} %get-tuple-element.211, ...), kind=kLoop, calls=%fused_computation.10.clone.1 | loop fusion | flops 1572864 | bytes 8126464 | tf_op jit(solution)/shard_map/while/body/eval_jaxpr/reduce_sum | solution.py:38
  137.0 3.4 %all-to-all-start.1 = ((f32[8,8,384]{2,1,0:T(8,128)}), f32[8,8,384]{2,1,0:T(8,128)S(1)}, u32[]{:S(2)}, u32[]{:S(2)}) async-start(f32[8,8,384]{2,1,0:T(8,128)} %bitcast.5), calls=%async_computation.1 | async-start | bytes 196608 | tf_op jit(solution)/shard_map/all_to_all | solution.py:120
  140.6 4.9 %all-to-all-done.1 = f32[8,8,384]{2,1,0:T(8,128)S(1)} async-done(((f32[8,8,384]{2,1,0:T(8,128)}), f32[8,8,384]{2,1,0:T(8,128)S(1)}, u32[]{:S(2)}, u32[]{:S(2)}) %all-to-all-start.1) | async-done | bytes 98336 | tf_op jit(solution)/shard_map/all_to_all | solution.py:120
  146.8 18.7 %psum.7 = f32[6,3,64]{2,0,1:T(8,128)S(1)} all-reduce(f32[6,3,64]{2,0,1:T(8,128)S(1)} %bitcast.74), channel_id=1, replica_groups=mesh['loan'=8,'path'=4] {'path'}, use_global_device_ids=true, to_apply=%region_7.8 | all-reduce | flops 1152 | bytes 9216 | tf_op jit(solution)/shard_map/psum | solution.py:141
  (192 shorter events, 69.3 us)
Async XLA Ops:
  7.2 14.3 %copy-start.9 = (s32[2,32]{1,0:T(2,128)S(1)}, s32[2,32]{1,0:T(2,128)}, u32[]{:S(2)}) copy-start(s32[2,32]{1,0:T(2,128)} %param.14) | copy-start | bytes 772
  7.2 14.3 %copy-start.5 = (s32[64,6]{0,1:T(8,128)S(1)}, s32[64,6]{0,1:T(8,128)}, u32[]{:S(2)}) copy-start(s32[64,6]{0,1:T(8,128)} %param.23) | copy-start | bytes 4612
  7.2 14.4 %copy-start.7 = (s32[512]{0:T(512)S(1)}, s32[512]{0:T(512)}, u32[]{:S(2)}) copy-start(s32[512]{0:T(512)} %param.15) | copy-start | bytes 6148
  7.2 14.6 %copy-start.6 = (s32[512]{0:T(512)S(1)}, s32[512]{0:T(512)}, u32[]{:S(2)}) copy-start(s32[512]{0:T(512)} %param.18) | copy-start | bytes 6148
  7.2 14.6 %copy-start.8 = (f32[512]{0:T(512)S(1)}, f32[512]{0:T(512)}, u32[]{:S(2)}) copy-start(f32[512]{0:T(512)} %param.20) | copy-start | bytes 6148
  7.2 31.6 %all-gather.2.cloned.1.call-start = ((), (), s32[]{:S(2)}) async-start(), calls=%async_computation.3 | async-start | bytes 1916928 | tf_op jit(solution)/shard_map/all_gather | solution.py:75
  13.2 9.8 %all-to-all-start = ((f32[8,8,1]{1,2,0:T(1,128)}), f32[8,8,1]{1,2,0:T(1,128)S(1)}, u32[]{:S(2)}, u32[]{:S(2)}) async-start(f32[8,8,1]{1,2,0:T(1,128)} %bitcast), calls=%async_computation | async-start | bytes 8192 | tf_op jit(solution)/shard_map/all_to_all | solution.py:122
  23.0 7.9 %all-to-all-start.2 = ((f32[8,8,1]{1,2,0:T(1,128)}), f32[8,8,1]{1,2,0:T(1,128)S(1)}, u32[]{:S(2)}, u32[]{:S(2)}) async-start(f32[8,8,1]{1,2,0:T(1,128)} %bitcast.10), calls=%async_computation.2 | async-start | bytes 8192 | tf_op jit(solution)/shard_map/all_to_all | solution.py:121
  46.4 2.8 %copy-start = (f32[6,128,512]{2,1,0:T(8,128)}, f32[6,128,512]{2,1,0:T(8,128)S(1)}, u32[]{:S(2)}) copy-start(f32[6,128,512]{2,1,0:T(8,128)S(1)} %get-tuple-element.211) | copy-start | bytes 4718596 | tf_op jit(solution)/shard_map/while
  53.9 2.8 %copy-start = (f32[6,128,512]{2,1,0:T(8,128)}, f32[6,128,512]{2,1,0:T(8,128)S(1)}, u32[]{:S(2)}) copy-start(f32[6,128,512]{2,1,0:T(8,128)S(1)} %get-tuple-element.211) | copy-start | bytes 4718596 | tf_op jit(solution)/shard_map/while
  56.6 2.2 %copy-start.1 = (f32[5,128,512]{2,1,0:T(8,128)S(1)}, f32[5,128,512]{2,1,0:T(8,128)}, u32[]{:S(2)}) copy-start(f32[5,128,512]{2,1,0:T(8,128)} %get-tuple-element.213) | copy-start | bytes 3932164 | tf_op jit(solution)/shard_map/while
  61.4 2.8 %copy-start = (f32[6,128,512]{2,1,0:T(8,128)}, f32[6,128,512]{2,1,0:T(8,128)S(1)}, u32[]{:S(2)}) copy-start(f32[6,128,512]{2,1,0:T(8,128)S(1)} %get-tuple-element.211) | copy-start | bytes 4718596 | tf_op jit(solution)/shard_map/while
  64.1 2.2 %copy-start.1 = (f32[5,128,512]{2,1,0:T(8,128)S(1)}, f32[5,128,512]{2,1,0:T(8,128)}, u32[]{:S(2)}) copy-start(f32[5,128,512]{2,1,0:T(8,128)} %get-tuple-element.213) | copy-start | bytes 3932164 | tf_op jit(solution)/shard_map/while
  68.9 2.8 %copy-start = (f32[6,128,512]{2,1,0:T(8,128)}, f32[6,128,512]{2,1,0:T(8,128)S(1)}, u32[]{:S(2)}) copy-start(f32[6,128,512]{2,1,0:T(8,128)S(1)} %get-tuple-element.211) | copy-start | bytes 4718596 | tf_op jit(solution)/shard_map/while
  76.4 2.8 %copy-start = (f32[6,128,512]{2,1,0:T(8,128)}, f32[6,128,512]{2,1,0:T(8,128)S(1)}, u32[]{:S(2)}) copy-start(f32[6,128,512]{2,1,0:T(8,128)S(1)} %get-tuple-element.211) | copy-start | bytes 4718596 | tf_op jit(solution)/shard_map/while
  83.9 2.8 %copy-start = (f32[6,128,512]{2,1,0:T(8,128)}, f32[6,128,512]{2,1,0:T(8,128)S(1)}, u32[]{:S(2)}) copy-start(f32[6,128,512]{2,1,0:T(8,128)S(1)} %get-tuple-element.211) | copy-start | bytes 4718596 | tf_op jit(solution)/shard_map/while
  91.4 2.8 %copy-start = (f32[6,128,512]{2,1,0:T(8,128)}, f32[6,128,512]{2,1,0:T(8,128)S(1)}, u32[]{:S(2)}) copy-start(f32[6,128,512]{2,1,0:T(8,128)S(1)} %get-tuple-element.211) | copy-start | bytes 4718596 | tf_op jit(solution)/shard_map/while
  98.9 2.8 %copy-start = (f32[6,128,512]{2,1,0:T(8,128)}, f32[6,128,512]{2,1,0:T(8,128)S(1)}, u32[]{:S(2)}) copy-start(f32[6,128,512]{2,1,0:T(8,128)S(1)} %get-tuple-element.211) | copy-start | bytes 4718596 | tf_op jit(solution)/shard_map/while
  101.6 2.3 %copy-start.1 = (f32[5,128,512]{2,1,0:T(8,128)S(1)}, f32[5,128,512]{2,1,0:T(8,128)}, u32[]{:S(2)}) copy-start(f32[5,128,512]{2,1,0:T(8,128)} %get-tuple-element.213) | copy-start | bytes 3932164 | tf_op jit(solution)/shard_map/while
  106.4 2.8 %copy-start = (f32[6,128,512]{2,1,0:T(8,128)}, f32[6,128,512]{2,1,0:T(8,128)S(1)}, u32[]{:S(2)}) copy-start(f32[6,128,512]{2,1,0:T(8,128)S(1)} %get-tuple-element.211) | copy-start | bytes 4718596 | tf_op jit(solution)/shard_map/while
  113.9 2.8 %copy-start = (f32[6,128,512]{2,1,0:T(8,128)}, f32[6,128,512]{2,1,0:T(8,128)S(1)}, u32[]{:S(2)}) copy-start(f32[6,128,512]{2,1,0:T(8,128)S(1)} %get-tuple-element.211) | copy-start | bytes 4718596 | tf_op jit(solution)/shard_map/while
  121.4 2.8 %copy-start = (f32[6,128,512]{2,1,0:T(8,128)}, f32[6,128,512]{2,1,0:T(8,128)S(1)}, u32[]{:S(2)}) copy-start(f32[6,128,512]{2,1,0:T(8,128)S(1)} %get-tuple-element.211) | copy-start | bytes 4718596 | tf_op jit(solution)/shard_map/while
  128.9 2.8 %copy-start = (f32[6,128,512]{2,1,0:T(8,128)}, f32[6,128,512]{2,1,0:T(8,128)S(1)}, u32[]{:S(2)}) copy-start(f32[6,128,512]{2,1,0:T(8,128)S(1)} %get-tuple-element.211) | copy-start | bytes 4718596 | tf_op jit(solution)/shard_map/while
  137.0 8.5 %all-to-all-start.1 = ((f32[8,8,384]{2,1,0:T(8,128)}), f32[8,8,384]{2,1,0:T(8,128)S(1)}, u32[]{:S(2)}, u32[]{:S(2)}) async-start(f32[8,8,384]{2,1,0:T(8,128)} %bitcast.5), calls=%async_computation.1 | async-start | bytes 196608 | tf_op jit(solution)/shard_map/all_to_all | solution.py:120
  (12 other events, 22.0 us)
Sparse Core Ops, SparseCore 0:
  9.9 28.8 all-gather.1
where the time goes:
time: 174 us; the launch traced here: 173 us
  other arithmetic  81.9 us (47%)
  local copies, waits for them, and re-layouts  24 us (14%)
  blocking collectives  18.7 us (11%)
  waiting for transfers between devices  17.3 us (10%)
  between operations  14.2 us (8%)
  starting transfers between devices  11.9 us (7%)
  matrix products  4.24 us (2%)
    reduce_sum x12, other arithmetic, month_step(): first_state = state[0] * stay_rate[0] + jnp.sum(backward[1:], axis=0)  32.9 us
    dynamic_update_slice x12, other arithmetic, roll_months(): state_pair, history = lax.scan(month_step, (start_state, loss_start), level)  26.6 us
    psum x1, blocking collectives, shards(): expected_loss = lax.psum(partial_value, 'path') / path_count  18.7 us
    sub x12, other arithmetic, month_step(): stay_rate = (1.0 - roll_rate) * (1.0 - cure_rate)  14.8 us
    dynamic_slice x24, local copies, waits for them, and re-layouts, roll_months(): state_pair, history = lax.scan(month_step, (start_state, loss_start), level)  13.2 us
    all_gather x1, waiting for transfers between devices, shards(): shard = lax.all_gather(price_moves, 'loan', axis=1, tiled=True)  6.63 us
    all_to_all x1, starting transfers between devices, shards(): lax.all_to_all(outgoing[2], 'loan', split_axis=0, concat_axis=0, tiled=True)  5.2 us
    all_to_all x1, waiting for transfers between devices, shards(): lax.all_to_all(outgoing[0], 'loan', split_axis=0, concat_axis=0, tiled=True)  4.94 us
  transfers between devices with their start and end apart: 4, of which 4 were waited for; matrix products, arithmetic and copies ran while one was open for 5% of the time, Pallas kernels for 0%

commit v1 on v0

v1 whole, which is shorter than its diff:
```python
import functools

import jax
import jax.numpy as jnp
from jax import lax
from jax.experimental import pallas as pl
from jax.experimental.pallas import tpu as pltpu
from jax.sharding import PartitionSpec as P

BLOCK = 256
LANES = 128
STRESS = 0.3
F32 = jnp.float32
BF16 = jnp.bfloat16

VMEM = pl.BlockSpec(memory_space=pltpu.VMEM)
SMEM = pl.BlockSpec(memory_space=pltpu.SMEM)


def next_pow2(value):
    return 1 << (value - 1).bit_length()


class Sizes:
    def __init__(self, price_moves, block_regions, block_pools, attach_bps, hazard_base):
        self.devs = lax.axis_size("loan")
        self.path_devs = lax.axis_size("path")
        self.months, self.metros, self.paths = price_moves.shape
        self.blocks, self.regions = block_regions.shape
        self.slots = block_pools.shape[1]
        self.pools, self.tranches = attach_bps.shape
        self.live = hazard_base.shape[1]
        self.dates = self.months // 4
        self.width = self.paths // self.devs
        self.halves = 2
        self.half = self.width // self.halves
        self.pad = next_pow2(max(self.metros, 16))
        self.fold = LANES // self.pad
        self.groups = -(-self.months // self.fold)
        self.price_rows = self.groups * self.width
        self.loan_rows = self.blocks * BLOCK // LANES
        self.info_rows = -(-(10 * self.loan_rows + 2) // 16) * 16
        self.rows = self.price_rows + self.info_rows
        self.dev_slots = self.blocks * self.slots
        self.sources = LANES // self.dev_slots
        self.all_pools = self.pools * self.devs


def pieces(value, count):
    out = []
    for _ in range(count):
        piece = value.astype(BF16).astype(F32)
        out.append(piece)
        value = value - piece
    return out


def pack_kernel(z, moves, regions, pool_lists, region, pool, init, balance, ltv, out, info, table):
    me = lax.axis_index("loan")
    for g in range(z.groups):
        parts = []
        for h in range(z.fold):
            t = h * z.groups + g
            if t < z.months:
                block = moves[t].astype(F32)
            else:
                block = jnp.zeros((z.metros, z.paths), F32)
            parts.append(block)
            if z.pad > z.metros:
                parts.append(jnp.zeros((z.pad - z.metros, z.paths), F32))
        turned = jnp.concatenate(parts, axis=0).T
        step = z.paths // z.halves
        for k in range(z.devs):
            both = [turned[h * step + k * z.half : h * step + (k + 1) * z.half] for h in range(z.halves)]
            out[k, g * z.width : (g + 1) * z.width, :] = jnp.concatenate(both, axis=0).astype(BF16)
    info[...] = jnp.zeros_like(info)
    per = BLOCK // LANES
    for b in range(z.blocks):
        rows = slice(b * per, (b + 1) * per)
        slot = region[rows, :]
        metro = jnp.zeros(slot.shape, jnp.int32)
        for j in range(z.regions):
            metro = jnp.where(slot == j, regions[b, j], metro)
        owner = jnp.zeros(slot.shape, jnp.int32)
        for k in range(1, z.devs):
            owner = owner + jnp.where(metro >= k * z.metros, 1, 0)
        local = metro - owner * z.metros
        values = [owner.astype(F32), local.astype(F32), init[rows, :].astype(F32), pool[rows, :].astype(F32)]
        values += pieces(jnp.log(ltv[rows, :]), 3) + pieces(balance[rows, :], 3)
        for q, value in enumerate(values):
            info[q * z.loan_rows + b * per : q * z.loan_rows + (b + 1) * per, :] = value
    table[...] = jnp.zeros_like(table)
    table[0 : z.blocks, 0 : z.slots] = pool_lists[...].astype(F32)
    lists = table[...]
    row = lists[0:1, :]
    for b in range(1, z.blocks):
        row = row + pltpu.roll(lists, b * z.slots, 1)[b : b + 1, :]
    place = lax.broadcasted_iota(jnp.int32, (1, LANES), 1) // z.dev_slots
    wide = row
    for c in range(1, z.sources):
        wide = wide + pltpu.roll(jnp.broadcast_to(row, (8, LANES)), c * z.dev_slots, 1)[0:1, :]
    wide = jnp.where(place == lax.rem(me, z.sources), wide, 0.0)
    high = jnp.floor(wide * (1.0 / 64.0))
    info[10 * z.loan_rows : 10 * z.loan_rows + 1, :] = high
    info[10 * z.loan_rows + 1 : 10 * z.loan_rows + 2, :] = wide - 64.0 * high
    packed = info[...].astype(BF16)
    for k in range(z.devs):
        out[k, z.price_rows :, :] = packed


def rolled(value, shift):
    shift = shift % LANES
    return value if shift == 0 else pltpu.roll(value, shift, 1)


def months_kernel(z, got, base, slope, out, source_moves, moved, dated, sums, pool_rows, turned):
    lane = lax.broadcasted_iota(jnp.int32, (1, LANES), 1)
    for j in range(z.devs // z.fold):
        for h in range(z.fold):
            mixed = None
            count = min(z.groups, z.months - h * z.groups) * z.width
            if count <= 0:
                continue
            for i in range(z.fold):
                part = rolled(got[j * z.fold + i, 0 : z.price_rows, :].astype(F32), (i - h) * z.pad)
                mixed = part if mixed is None else jnp.where(lane // z.pad == i, part, mixed)
            source_moves[
                h * z.price_rows : h * z.price_rows + count, j * LANES : (j + 1) * LANES
            ] = mixed[0:count].astype(BF16)
    sums[...] = jnp.zeros_like(sums)
    pool_rows[...] = jnp.zeros_like(pool_rows)
    keys = z.devs * z.pad
    total_paths = z.paths * z.path_devs
    path = lax.broadcasted_iota(jnp.int32, (z.width, BLOCK), 0)
    here = (
        lax.axis_index("path") * z.paths
        + (path // z.half) * (z.paths // z.halves)
        + lax.axis_index("loan") * z.half
        + path % z.half
    )
    stress = STRESS * ((here.astype(F32) + 0.5) / float(total_paths)) / float(z.months)
    roll_base = [0.5 * base[0, s] for s in range(z.live)]
    roll_slope = [0.5 * slope[0, s] for s in range(z.live)]
    cure_base = [0.5 * base[1, s] for s in range(z.live)]
    cure_slope = [-0.5 * slope[1, s] for s in range(z.live)]
    per = BLOCK // LANES
    marks = z.dates * z.width

    def source_step(s, carry):
        info = got[s, z.price_rows :, :].astype(F32)
        group = s // z.sources
        pool_rows[group] = pool_rows[group] + info[10 * z.loan_rows : 10 * z.loan_rows + 2, :]

        for b in range(z.blocks):

            def row(q):
                first = q * z.loan_rows + b * per
                return jnp.concatenate([info[first + r : first + r + 1, :] for r in range(per)], axis=1)

            key = row(0) * float(z.pad) + row(1)
            iota = lax.broadcasted_iota(jnp.int32, (keys, BLOCK), 0).astype(F32)
            chooser = jnp.where(iota == key, 1.0, 0.0).astype(BF16)
            moved[...] = jnp.dot(source_moves[...], chooser, preferred_element_type=F32)
            start = row(2)
            balance_rows = [row(7), row(8), row(9)]
            balance = balance_rows[0] + balance_rows[1] + balance_rows[2]
            level = jnp.broadcast_to(row(4) + row(5) + row(6), (z.width, BLOCK))
            state = [
                jnp.broadcast_to(jnp.where(start == float(k), 1.0, 0.0), (z.width, BLOCK))
                for k in range(z.live)
            ]
            loss = jnp.zeros((z.width, BLOCK), F32)
            for t in range(z.months):
                level = level + (stress - moved[t * z.width : (t + 1) * z.width, :])
                ahead = []
                keep = []
                back = None
                for k in range(z.live):
                    roll = jnp.tanh(roll_base[k] + roll_slope[k] * level)
                    cure = jnp.tanh(cure_base[k] + cure_slope[k] * level)
                    part = state[k] * roll
                    ahead.append(state[k] + part)
                    rest = state[k] - part
                    cured = rest * cure
                    keep.append(rest - cured)
                    if k > 0:
                        gain = rest + cured
                        back = gain if back is None else back + gain
                scale = 0.5 * 0.25**t
                severity = 0.35 * scale + (0.25 * scale) * jnp.tanh(1.5 * level)
                loss = loss + severity * ahead[z.live - 1]
                state = [keep[0] + back] + [
                    2.0 * ahead[k - 1] + keep[k] for k in range(1, z.live)
                ]
                if t % 4 == 3:
                    d = t // 4
                    high, low = pieces(balance * loss, 2)
                    dated[d * z.width : (d + 1) * z.width, :] = high.astype(BF16)
                    dated[marks + d * z.width : marks + (d + 1) * z.width, :] = low.astype(BF16)
            money = jnp.concatenate(balance_rows + [jnp.zeros((13, BLOCK), F32)], axis=0)
            dated[2 * marks :, :] = money.astype(BF16)
            place = lax.rem(s, z.sources) * z.dev_slots + b * z.slots
            slot = row(3) + place.astype(F32)
            slot_iota = lax.broadcasted_iota(jnp.int32, (LANES, BLOCK), 0).astype(F32)
            members = jnp.where(slot_iota == slot, 1.0, 0.0).astype(BF16)
            sums[group] = sums[group] + lax.dot_general(
                dated[...], members, (((1,), (1,)), ((), ())), preferred_element_type=F32
            )
        return carry

    lax.fori_loop(0, z.devs, source_step, 0)

    for group in range(z.devs // z.sources):
        total = sums[group]
        money = total[2 * marks : 2 * marks + 1] + total[2 * marks + 1 : 2 * marks + 2]
        money = money + total[2 * marks + 2 : 2 * marks + 3]
        ratio = (total[0:marks] + total[marks : 2 * marks]) / money
        split = jnp.concatenate(pieces(ratio, 3), axis=0).astype(BF16)
        listed = pool_rows[group]
        pool_id = listed[0:1] * 64.0 + listed[1:2]
        pool_iota = lax.broadcasted_iota(jnp.int32, (z.all_pools, LANES), 0).astype(F32)
        order = jnp.where(pool_iota == pool_id, 1.0, 0.0).astype(BF16)
        part = lax.dot_general(
            split, order, (((1,), (1,)), ((), ())), preferred_element_type=F32
        )
        turned[...] = part if group == 0 else turned[...] + part
    ratio = turned[0:marks, :] + turned[marks : 2 * marks, :] + turned[2 * marks : 3 * marks, :]
    wide = LANES // z.pools
    for k in range(z.devs):
        both = ratio[:, (k // wide) * LANES : (k // wide + 1) * LANES]
        own = k % wide
        for d in range(z.dates):
            mixed = None
            for h in range(z.halves):
                first = d * z.width + h * z.half
                part = rolled(both[first : first + z.half], (h - own) * z.pools)
                mixed = part if mixed is None else jnp.where(lane // z.pools == h, part, mixed)
            out[k, d * z.half : (d + 1) * z.half, :] = mixed


def steps_of(z, bps):
    attach = bps.astype(F32) / 10000.0
    top = jnp.concatenate([attach[:, 1:], jnp.ones((z.pools, 1), F32)], axis=1)
    return attach, top - attach


def means_kernel(z, got, bps, out, scratch):
    attach, height = steps_of(z, bps[...])
    scratch[...] = jnp.zeros_like(scratch)
    scratch[0 : z.pools, 0 : z.tranches] = attach
    scratch[0 : z.pools, 8 : 8 + z.tranches] = height
    for h in range(1, z.halves):
        scratch[h * z.pools : (h + 1) * z.pools, 0:16] = scratch[0 : z.pools, 0:16]
    rows = scratch[...].T
    out[...] = jnp.zeros_like(out)
    for d in range(z.dates):
        ratio = jnp.concatenate(
            [got[k, d * z.half : (d + 1) * z.half, :] for k in range(z.devs)], axis=0
        )
        for j in range(z.tranches):
            share = jnp.clip((ratio - rows[j : j + 1]) / rows[8 + j : 9 + j], 0.0, 1.0)
            out[j * z.dates + d : j * z.dates + d + 1, :] = jnp.sum(share, axis=0, keepdims=True)


def paths_kernel(z, got, bps, out):
    attach, height = steps_of(z, bps[...])
    d = z.dates - 1
    ratio = jnp.concatenate(
        [got[k, d * z.half : (d + 1) * z.half, :] for k in range(z.devs)], axis=0
    )
    side = z.paths // z.halves
    turned = ratio.T
    ratio = jnp.concatenate(
        [turned[h * z.pools : (h + 1) * z.pools, 0:side] for h in range(z.halves)], axis=1
    )
    for j in range(z.tranches):
        share = (ratio - attach[:, j : j + 1]) / height[:, j : j + 1]
        out[j] = jnp.clip(share, 0.0, 1.0)


def shards(
    price_moves,
    block_regions,
    region_slot,
    block_pools,
    pool_slot,
    init_state,
    balance,
    loan_to_value,
    hazard_base,
    hazard_slope,
    attach_bps,
):
    z = Sizes(price_moves, block_regions, block_pools, attach_bps, hazard_base)

    def lanes(value):
        return value.reshape(z.loan_rows, LANES)

    sent = pl.pallas_call(
        functools.partial(pack_kernel, z),
        out_shape=jax.ShapeDtypeStruct((z.devs, z.rows, LANES), BF16),
        in_specs=[VMEM, SMEM] + [VMEM] * 6,
        out_specs=VMEM,
        scratch_shapes=[pltpu.VMEM((z.info_rows, LANES), F32), pltpu.VMEM((8, LANES), F32)],
        name="pack",
    )(
        price_moves,
        block_regions,
        block_pools,
        lanes(region_slot),
        lanes(pool_slot),
        lanes(init_state),
        lanes(balance),
        lanes(loan_to_value),
    )
    got = lax.all_to_all(sent, "loan", 0, 0, tiled=True)
    marks = z.dates * z.width
    slot_groups = z.devs // z.sources
    ratios = pl.pallas_call(
        functools.partial(months_kernel, z),
        out_shape=jax.ShapeDtypeStruct((z.devs, z.dates * z.half, LANES), F32),
        in_specs=[VMEM, SMEM, SMEM],
        out_specs=VMEM,
        scratch_shapes=[
            pltpu.VMEM((z.months * z.width, z.devs * z.pad), BF16),
            pltpu.VMEM((z.months * z.width, BLOCK), F32),
            pltpu.VMEM((2 * marks + 16, BLOCK), BF16),
            pltpu.VMEM((slot_groups, 2 * marks + 16, LANES), F32),
            pltpu.VMEM((slot_groups, 2, LANES), F32),
            pltpu.VMEM((3 * marks, z.all_pools), F32),
        ],
        name="months",
    )(got, hazard_base, hazard_slope)
    owned = lax.all_to_all(ratios, "loan", 0, 0, tiled=True)
    total_rows = -(-z.tranches * z.dates // 8) * 8
    sums = pl.pallas_call(
        functools.partial(means_kernel, z),
        out_shape=jax.ShapeDtypeStruct((total_rows, LANES), F32),
        in_specs=[VMEM, VMEM],
        out_specs=VMEM,
        scratch_shapes=[pltpu.VMEM((LANES, LANES), F32)],
        name="means",
    )(owned, attach_bps)
    terms = [sums] + [
        lax.ppermute(sums, "path", [(i, i ^ k) for i in range(z.path_devs)])
        for k in range(1, z.path_devs)
    ]
    path_loss = pl.pallas_call(
        functools.partial(paths_kernel, z),
        out_shape=jax.ShapeDtypeStruct((z.tranches, z.pools, z.paths), F32),
        in_specs=[VMEM, VMEM],
        out_specs=VMEM,
        name="paths",
    )(owned, attach_bps)
    while len(terms) > 1:
        terms = [terms[i] + terms[i + 1] for i in range(0, len(terms), 2)]
    total = terms[0][: z.tranches * z.dates]
    total = sum(total[:, h * z.pools : (h + 1) * z.pools] for h in range(z.halves))
    expected_loss = (total / (z.paths * z.path_devs)).reshape(z.tranches, z.dates, z.pools)
    return expected_loss, path_loss


def solution(mesh):
    in_specs = (
        P(None, "loan", "path"),
        P("loan", None),
        P("loan"),
        P("loan", None),
        P("loan"),
        P("loan"),
        P("loan"),
        P("loan"),
        P(),
        P(),
        P("loan", None),
    )
    out_specs = (P(None, None, "loan"), P(None, "loan", "path"))
    return jax.shard_map(shards, mesh=mesh, in_specs=in_specs, out_specs=out_specs, check_vma=False)
```

time: 174 us -> 49.8 us (0.29)
  other arithmetic: 81.9 us -> 0.08 us
  local copies, waits for them, and re-layouts: 24 us -> 1.96 us
  Pallas kernels: 0 us -> 18 us
  between operations: 14.2 us -> 0.66 us
  waiting for transfers between devices: 17.3 us -> 8.22 us
  blocking collectives: 18.7 us -> 12.6 us
  matrix products: 4.24 us -> 0 us
  starting transfers between devices: 11.9 us -> 7.88 us
    reduce_sum x13 -> x0, other arithmetic: 33 us -> none  [the longest x12 32.9 us: month_step(): first_state = state[0] * stay_rate[0] + jnp.sum(backward[1:], axis=0)]
    dynamic_update_slice x12 -> x0, other arithmetic: 26.6 us -> none  [roll_months(): state_pair, history = lax.scan(month_step, (start_state, loss_start), level)]
    psum x1 -> x0, blocking collectives: 18.7 us -> none  [shards(): expected_loss = lax.psum(partial_value, 'path') / path_count]
    pallas_call x0 -> x4, Pallas kernels: none -> 18 us  [the longest x1 12.5 us: shards(): pl.pallas_call(functools.partial(months_kernel, z), out_shape=jax.ShapeDt...]
    sub x13 -> x0, other arithmetic: 14.8 us -> none  [the longest x12 14.8 us: month_step(): stay_rate = (1.0 - roll_rate) * (1.0 - cure_rate)]
    dynamic_slice x24 -> x0, local copies, waits for them, and re-layouts: 13.2 us -> none  [roll_months(): state_pair, history = lax.scan(month_step, (start_state, loss_start), level)]
    all_to_all x0 -> x1, blocking collectives: none -> 12.6 us  [shards(): got = lax.all_to_all(sent, 'loan', 0, 0, tiled=True)]
    all_to_all x3 -> x1, starting transfers between devices: 11.9 us -> 3.49 us  [shards(): owned = lax.all_to_all(ratios, 'loan', 0, 0, tiled=True)]
  transfers between devices with their start and end apart: 4 -> 4, of which waited for: 4 -> 3; matrix products, arithmetic and copies ran while one was open for 5% -> 1% of each run, Pallas kernels for 0% -> 4%
where the time goes in v1:
time: 49.8 us; the launch traced here: 49.4 us
  Pallas kernels  18 us (36%)
  blocking collectives  12.6 us (25%)
  waiting for transfers between devices  8.22 us (17%)
  starting transfers between devices  7.88 us (16%)
  local copies, waits for them, and re-layouts  1.96 us (4%)
  between operations  0.66 us (1%)
    all_to_all x1, blocking collectives, shards(): got = lax.all_to_all(sent, 'loan', 0, 0, tiled=True)  12.6 us
    pallas_call x1, Pallas kernels, shards(): pl.pallas_call(functools.partial(months_kernel, z), out_shape=jax.ShapeDt...  12.5 us
    all_to_all x1, waiting for transfers between devices, shards(): owned = lax.all_to_all(ratios, 'loan', 0, 0, tiled=True)  4.41 us
    ppermute x3, starting transfers between devices, shards(): lax.ppermute(sums, 'path', [(i, i ^ k) for i in range(z.path_devs)])  4.39 us
    ppermute x3, waiting for transfers between devices, shards(): lax.ppermute(sums, 'path', [(i, i ^ k) for i in range(z.path_devs)])  3.81 us
    all_to_all x1, starting transfers between devices, shards(): owned = lax.all_to_all(ratios, 'loan', 0, 0, tiled=True)  3.49 us
    pallas_call x1, Pallas kernels, shards(): pl.pallas_call(functools.partial(pack_kernel, z), out_shape=jax.ShapeDtyp...  1.89 us
    pallas_call x1, Pallas kernels, shards(): pl.pallas_call(functools.partial(paths_kernel, z), out_shape=jax.ShapeDty...  1.88 us
  transfers between devices with their start and end apart: 4, of which 3 were waited for; matrix products, arithmetic and copies ran while one was open for 1% of the time, Pallas kernels for 4%

profile of v1, /device:TPU:0, one launch (start us, length us, event | category | flops | bytes accessed | tf_op | source)
XLA Modules:
  0.0 49.4 jit_solution(15666111627294683902)
XLA Ops:
  0.6 1.9 %pack.1 = bf16[8,144,128]{2,1,0:T(8,128)(2,1)} custom-call(bf16[12,52,128]{2,1,0:T(8,128)(2,1)} %moves.1, s32[2,32]{1,0:T(2,128)} %regions.1, s32[2,32]{1,0:T(2,128)} %pool_lists.1, s32[4,128]{1,0:T(4,128)} %bitcast.5, s32[4,128]{1,0:T(4,128)} %bitcast.6, s32[4,128]{1,0:T(4,128)} %bitcast.7, f32[4,128]{1,0:T(4,128)} %bitcast.8, f32[4,128]{1,0:T(4,128)} %bitcast.9), custom_call_target="tpu_custom_call" | custom-call | tf_op jit(solution)/shard_map/pack/pallas_call | solution.py:299
  2.5 12.6 %all_to_all.10.got = bf16[8,144,128]{2,1,0:T(8,128)(2,1)} all-to-all(bf16[8,144,128]{2,1,0:T(8,128)(2,1)} %pack.1), channel_id=1, replica_groups=mesh['loan'=8,'path'=4] {'loan'}, dimensions={0} | all-to-all | bytes 589824 | tf_op jit(solution)/shard_map/all_to_all | solution.py:316
  15.1 12.5 %months.1 = f32[8,24,128]{2,1,0:T(8,128)} custom-call(bf16[8,144,128]{2,1,0:T(8,128)(2,1)} %all_to_all.10.got, f32[2,6]{1,0:T(2,128)} %base.1, f32[2,6]{1,0:T(2,128)} %slope.1), custom_call_target="tpu_custom_call" | custom-call | tf_op jit(solution)/shard_map/months/pallas_call | solution.py:319
  27.5 0.0 copy-start.2
  27.5 3.5 %all-to-all-start.1 = ((f32[8,24,128]{2,1,0:T(8,128)}), f32[8,24,128]{2,1,0:T(8,128)S(1)}, u32[]{:S(2)}, u32[]{:S(2)}) async-start(f32[8,24,128]{2,1,0:T(8,128)} %months.1), calls=%async_computation.1 | async-start | bytes 196608 | tf_op jit(solution)/shard_map/all_to_all | solution.py:334
  31.0 0.0 copy-done.2
  31.0 0.7 %copy.13.bps = s32[64,6]{1,0:T(8,128)} copy(s32[64,6]{0,1:T(8,128)S(1)} %copy-done.2) | data formatting | bytes 3072 | tf_op args[10]
  31.7 4.4 %all-to-all-done.1.got = f32[8,24,128]{2,1,0:T(8,128)S(1)} async-done(((f32[8,24,128]{2,1,0:T(8,128)}), f32[8,24,128]{2,1,0:T(8,128)S(1)}, u32[]{:S(2)}, u32[]{:S(2)}) %all-to-all-start.1) | async-done | bytes 98336 | tf_op jit(solution)/shard_map/all_to_all | solution.py:334
  36.2 0.0 copy-start
  36.2 0.6 %copy-done = f32[8,24,128]{2,1,0:T(8,128)} copy-done((f32[8,24,128]{2,1,0:T(8,128)}, f32[8,24,128]{2,1,0:T(8,128)S(1)}, u32[]{:S(2)}) %copy-start) | copy-done | bytes 98328
  36.8 1.8 %means.1 = f32[24,128]{1,0:T(8,128)} custom-call(f32[8,24,128]{2,1,0:T(8,128)} %copy-done, s32[64,6]{1,0:T(8,128)} %copy.13.bps), custom_call_target="tpu_custom_call" | custom-call | tf_op jit(solution)/shard_map/means/pallas_call | solution.py:336
  38.6 0.0 copy-start.1
  38.6 1.8 %collective-permute-start = (f32[24,128]{1,0:T(8,128)}, f32[24,128]{1,0:T(8,128)S(1)}, u32[]{:S(2)}, u32[]{:S(2)}) collective-permute-start(f32[24,128]{1,0:T(8,128)} %means.1), channel_id=1, source_target_pairs={{0,1},{1,0},{2,3},{3,2},{4,5},{5,4},{6,7},{7,6},{8,9},{9,8},{10,11... | collective-permute-start | bytes 36872 | tf_op jit(solution)/shard_map/ppermute | solution.py:345
  40.4 2.6 %collective-permute-start.1 = (f32[24,128]{1,0:T(8,128)}, f32[24,128]{1,0:T(8,128)S(1)}, u32[]{:S(2)}, u32[]{:S(2)}) collective-permute-start(f32[24,128]{1,0:T(8,128)} %means.1), channel_id=1, source_target_pairs={{0,2},{1,3},{2,0},{3,1},{4,6},{5,7},{6,4},{7,5},{8,10},{9,11},{10,... | collective-permute-start | bytes 36872 | tf_op jit(solution)/shard_map/ppermute | solution.py:345
  43.0 0.0 collective-permute-start.2
  43.0 1.9 %paths.1 = f32[6,64,128]{2,1,0:T(8,128)} custom-call(f32[8,24,128]{2,1,0:T(8,128)} %copy-done, s32[64,6]{1,0:T(8,128)} %copy.13.bps), custom_call_target="tpu_custom_call" | custom-call | tf_op jit(solution)/shard_map/paths/pallas_call | solution.py:348
  44.9 0.0 collective-permute-done
  44.9 0.3 collective-permute-done.1
  45.2 3.5 %collective-permute-done.2 = f32[24,128]{1,0:T(8,128)S(1)} collective-permute-done((f32[24,128]{1,0:T(8,128)}, f32[24,128]{1,0:T(8,128)S(1)}, u32[]{:S(2)}, u32[]{:S(2)}) %collective-permute-start.2) | collective-permute-done | bytes 12320 | tf_op jit(solution)/shard_map/ppermute | solution.py:345
  48.7 0.0 copy-done.1
  48.7 0.1 fusion
  48.8 0.6 %reshape.27 = f32[6,3,64]{2,1,0:T(4,128)} reshape(f32[18,64]{1,0:T(8,128)S(1)} %fusion) | data formatting | bytes 9216 | tf_op jit(solution)/shard_map/reshape | solution.py:359
  (1 shorter events, 0.0 us)
Async XLA Ops:
  27.5 3.5 %copy-start.2 = (s32[64,6]{0,1:T(8,128)S(1)}, s32[64,6]{0,1:T(8,128)}, u32[]{:S(2)}) copy-start(s32[64,6]{0,1:T(8,128)} %param.21) | copy-start | bytes 4612
  27.5 8.6 %all-to-all-start.1 = ((f32[8,24,128]{2,1,0:T(8,128)}), f32[8,24,128]{2,1,0:T(8,128)S(1)}, u32[]{:S(2)}, u32[]{:S(2)}) async-start(f32[8,24,128]{2,1,0:T(8,128)} %months.1), calls=%async_computation.1 | async-start | bytes 196608 | tf_op jit(solution)/shard_map/all_to_all | solution.py:334
  36.2 0.6 %copy-start = (f32[8,24,128]{2,1,0:T(8,128)}, f32[8,24,128]{2,1,0:T(8,128)S(1)}, u32[]{:S(2)}) copy-start(f32[8,24,128]{2,1,0:T(8,128)S(1)} %all-to-all-done.1.got) | copy-start | bytes 294916
  38.6 10.1 %copy-start.1 = (f32[24,128]{1,0:T(8,128)S(1)}, f32[24,128]{1,0:T(8,128)}, u32[]{:S(2)}) copy-start(f32[24,128]{1,0:T(8,128)} %means.1) | copy-start | bytes 36868
  38.6 6.3 %collective-permute-start = (f32[24,128]{1,0:T(8,128)}, f32[24,128]{1,0:T(8,128)S(1)}, u32[]{:S(2)}, u32[]{:S(2)}) collective-permute-start(f32[24,128]{1,0:T(8,128)} %means.1), channel_id=1, source_target_pairs={{0,1},{1,0},{2,3},{3,2},{4,5},{5,4},{6,7},{7,6},{8,9},{9,8},{10,11... | collective-permute-start | bytes 36872 | tf_op jit(solution)/shard_map/ppermute | solution.py:345
  40.4 4.8 %collective-permute-start.1 = (f32[24,128]{1,0:T(8,128)}, f32[24,128]{1,0:T(8,128)S(1)}, u32[]{:S(2)}, u32[]{:S(2)}) collective-permute-start(f32[24,128]{1,0:T(8,128)} %means.1), channel_id=1, source_target_pairs={{0,2},{1,3},{2,0},{3,1},{4,6},{5,7},{6,4},{7,5},{8,10},{9,11},{10,... | collective-permute-start | bytes 36872 | tf_op jit(solution)/shard_map/ppermute | solution.py:345
  43.0 5.7 %collective-permute-start.2 = (f32[24,128]{1,0:T(8,128)}, f32[24,128]{1,0:T(8,128)S(1)}, u32[]{:S(2)}, u32[]{:S(2)}) collective-permute-start(f32[24,128]{1,0:T(8,128)} %means.1), channel_id=1, source_target_pairs={{0,3},{1,2},{2,1},{3,0},{4,7},{5,6},{6,5},{7,4},{8,11},{9,10},{10,... | collective-permute-start | bytes 36872 | tf_op jit(solution)/shard_map/ppermute | solution.py:345

commit v2 on v1

v2 whole, which is shorter than its diff:
```python
import functools

import jax
import jax.numpy as jnp
from jax import lax
from jax.experimental import pallas as pl
from jax.experimental.pallas import tpu as pltpu
from jax.sharding import PartitionSpec as P

BLOCK = 256
LANES = 128
STRESS = 0.3
F32 = jnp.float32
BF16 = jnp.bfloat16

VMEM = pl.BlockSpec(memory_space=pltpu.VMEM)
SMEM = pl.BlockSpec(memory_space=pltpu.SMEM)


def next_pow2(value):
    return 1 << (value - 1).bit_length()


class Sizes:
    def __init__(self, price_moves, block_regions, block_pools, attach_bps, hazard_base):
        self.devs = lax.axis_size("loan")
        self.path_devs = lax.axis_size("path")
        self.chips = self.devs // 2
        self.months, self.metros, self.paths = price_moves.shape
        self.blocks, self.regions = block_regions.shape
        self.slots = block_pools.shape[1]
        self.pools, self.tranches = attach_bps.shape
        self.live = hazard_base.shape[1]
        self.dates = self.months // 4
        self.width = self.paths // self.devs
        self.halves = 2
        self.half = self.width // self.halves
        self.side = self.paths // self.halves
        self.pad = next_pow2(max(self.metros, 16))
        self.fold = LANES // self.pad
        self.groups = -(-self.months // self.fold)
        self.price_rows = self.groups * self.width
        self.per = BLOCK // LANES
        self.loan_rows = self.blocks * self.per
        self.list_row = 7 * self.loan_rows
        self.info_rows = -(-(self.list_row + 4) // 16) * 16
        self.rows = self.price_rows + self.info_rows
        self.dev_slots = self.blocks * self.slots
        self.sources = LANES // self.dev_slots
        self.all_pools = self.pools * self.devs
        self.slot_groups = self.devs // self.sources
        self.out_rows = self.dates * self.half
        self.steps = self.months * self.width

    def reach(self, state):
        return self.months - (self.live - 1 - state)


def pieces(value, count):
    out = []
    for _ in range(count):
        piece = value.astype(BF16).astype(F32)
        out.append(piece)
        value = value - piece
    return out


def rolled(value, shift):
    shift = shift % LANES
    return value if shift == 0 else pltpu.roll(value, shift, 1)


def pack_kernel(z, *refs):
    sources, (kept, passed), scratch = refs[:8], refs[8:10], refs[10:]
    moves, regions, pool_lists, region, pool, init, balance, ltv = scratch[:8]
    turned, info, table, arrived = scratch[8:]
    copies = [
        pltpu.make_async_copy(source, target, arrived.at[i])
        for i, (source, target) in enumerate(zip(sources, scratch[:8]))
    ]
    for copy in copies:
        copy.start()
    for copy in copies:
        copy.wait()
    me = lax.axis_index("loan")
    for g in range(z.groups):
        parts = []
        for h in range(z.fold):
            t = h * z.groups + g
            if t < z.months:
                parts.append(moves[t].astype(F32))
            else:
                parts.append(jnp.zeros((z.metros, z.paths), F32))
            if z.pad > z.metros:
                parts.append(jnp.zeros((z.pad - z.metros, z.paths), F32))
        turned[g] = jnp.concatenate(parts, axis=0).T
    for c in range(z.chips):
        for other, out in enumerate((kept, passed)):
            to = me ^ (2 * c + other)
            for g in range(z.groups):
                both = [
                    turned[g, pl.ds(h * z.side + to * z.half, z.half), :] for h in range(z.halves)
                ]
                first = c * z.rows + g * z.width
                out[first : first + z.width, :] = jnp.concatenate(both, axis=0).astype(BF16)
    info[...] = jnp.zeros_like(info)
    values = [region[...].astype(F32), init[...].astype(F32), pool[...].astype(F32)]
    values += pieces(jnp.log(ltv[...]), 2) + pieces(balance[...], 2)
    for q, value in enumerate(values):
        info[q * z.loan_rows : (q + 1) * z.loan_rows, :] = value
    lane = lax.broadcasted_iota(jnp.int32, (1, LANES), 1)
    mine = lane // z.dev_slots == lax.rem(me, z.sources)

    def spread(lists):
        table[...] = jnp.zeros_like(table)
        table[0 : z.blocks, 0 : z.slots] = lists.astype(F32)
        wide = table[...]
        row = wide[0:1, :]
        for b in range(1, z.blocks):
            row = row + pltpu.roll(wide, b * z.slots, 1)[b : b + 1, :]
        wide = row
        for c in range(1, z.sources):
            wide = wide + pltpu.roll(jnp.broadcast_to(row, (8, LANES)), c * z.dev_slots, 1)[0:1, :]
        return jnp.where(mine, wide, 0.0)

    listed = spread(pool_lists[...])
    high = jnp.floor(listed * (1.0 / 64.0))
    metro = spread(regions[...])
    owner = jnp.zeros_like(metro)
    for k in range(1, z.devs):
        owner = owner + jnp.where(metro >= float(k * z.metros), 1.0, 0.0)
    rows = [high, listed - 64.0 * high, owner, metro - owner * float(z.metros)]
    for i, row in enumerate(rows):
        info[z.list_row + i : z.list_row + i + 1, :] = row
    packed = info[...].astype(BF16)
    for c in range(z.chips):
        kept[c * z.rows + z.price_rows : (c + 1) * z.rows, :] = packed
        passed[c * z.rows + z.price_rows : (c + 1) * z.rows, :] = packed


def pair_kernel(z, rows, kept, passed, *outs):
    for c in range(1, z.chips):
        outs[c - 1][0:rows, :] = kept[c * rows : (c + 1) * rows, :]
        outs[c - 1][rows : 2 * rows, :] = passed[c * rows : (c + 1) * rows, :]


def part_of(z, own, others, j, rows):
    c, other = j // 2, j % 2
    if c == 0:
        return own[other], 0
    return others[c - 1], other * rows


def months_kernel(z, *refs):
    own, others = refs[:2], refs[2 : z.chips + 1]
    base, slope, kept, passed = refs[z.chips + 1 : z.chips + 5]
    (
        source_moves,
        info,
        both_pieces,
        moved_even,
        moved_odd,
        dated,
        sums,
        lists,
        ratios,
    ) = refs[z.chips + 5 :]
    me = lax.axis_index("loan")
    lane = lax.broadcasted_iota(jnp.int32, (1, LANES), 1)

    for j in range(z.devs // z.fold):
        parts = []
        for i in range(z.fold):
            ref, first = part_of(z, own, others, j * z.fold + i, z.rows)
            parts.append(ref[first : first + z.price_rows, :].astype(F32))
        for h in range(z.fold):
            mixed = None
            count = min(z.groups, z.months - h * z.groups) * z.width
            if count <= 0:
                continue
            for i in range(z.fold):
                part = rolled(parts[i], (i - h) * z.pad)
                mixed = part if mixed is None else jnp.where(lane // z.pad == i, part, mixed)
            first = h * z.price_rows
            source_moves[first : first + count, j * LANES : (j + 1) * LANES] = mixed[
                0:count
            ].astype(BF16)
    for j in range(z.devs):
        ref, first = part_of(z, own, others, j, z.rows)
        info[j] = ref[first + z.price_rows : first + z.rows, :].astype(F32)
    for group in range(z.slot_groups):
        total = info[group * z.sources, z.list_row : z.list_row + 4, :]
        for i in range(1, z.sources):
            total = total + info[group * z.sources + i, z.list_row : z.list_row + 4, :]
        lists[group] = total

    keys = z.devs * z.pad
    path = lax.broadcasted_iota(jnp.int32, (z.width, LANES), 0)
    here = (
        lax.axis_index("path") * z.paths
        + (path // z.half) * z.side
        + me * z.half
        + path % z.half
    )
    total_paths = float(z.paths * z.path_devs)
    stress = STRESS * ((here.astype(F32) + 0.5) / total_paths) / float(z.months)
    key_row = lax.broadcasted_iota(jnp.int32, (keys, LANES), 0).astype(F32)
    for group in range(z.slot_groups):
        listed = lists[group].astype(jnp.int32)
        key = ((listed[2:3] ^ me) * z.pad + listed[3:4]).astype(F32)
        chooser = jnp.where(key_row == key, 1.0, 0.0).astype(BF16)
        moved = jnp.dot(source_moves[...], chooser, preferred_element_type=F32)
        level = jnp.zeros((z.width, LANES), F32)
        highs, lows = [], []
        for t in range(z.months):
            level = level + (stress - moved[t * z.width : (t + 1) * z.width])
            high, low = pieces(level, 2)
            highs.append(high)
            lows.append(low)
        both_pieces[group, :, 0:LANES] = jnp.concatenate(highs, axis=0).astype(BF16)
        both_pieces[group, :, LANES:] = jnp.concatenate(lows, axis=0).astype(BF16)
    roll_base = [0.5 * base[0, k] for k in range(z.live)]
    roll_rate = [0.5 * slope[0, k] for k in range(z.live)]
    cure_base = [0.5 * base[1, k] for k in range(z.live)]
    cure_rate = [-0.5 * slope[1, k] for k in range(z.live)]
    sums[...] = jnp.zeros_like(sums)
    marks = z.dates * z.width
    slot_row = lax.broadcasted_iota(jnp.int32, (z.regions, BLOCK), 0).astype(F32)

    def row(j, b, q):
        first = q * z.loan_rows + b * z.per
        both = info[j, first : first + z.per, :]
        return jnp.concatenate([both[r : r + 1, :] for r in range(z.per)], axis=1)

    def one_hot(j, b, q):
        ours = jnp.where(slot_row == row(j, b, q), 1.0, 0.0)
        place = lax.rem(me ^ j, z.sources)
        parts = []
        for i in range(z.sources):
            here = jnp.where(place == i, ours, 0.0).astype(BF16)
            parts += [here if k == b else jnp.zeros_like(here) for k in range(z.blocks)]
        return jnp.concatenate(parts, axis=0)

    def fill(j, b, moved):
        chosen = one_hot(j, b, 0)
        chosen = jnp.concatenate([chosen, chosen], axis=0)
        moved[...] = jnp.dot(both_pieces[j // z.sources], chosen, preferred_element_type=F32)

    def run(j, b, moved):
        start = row(j, b, 1)
        begins = [start == float(k) for k in range(z.live)]
        ltv = row(j, b, 3) + row(j, b, 4)
        balance_rows = [row(j, b, q) for q in (5, 6)]
        balance = balance_rows[0] + balance_rows[1]

        def of_start(values):
            chosen = jnp.full((1, BLOCK), values[0], F32)
            for k in range(1, z.live):
                chosen = jnp.where(begins[k], values[k], chosen)
            return chosen

        state = None
        loss = jnp.zeros((z.width, BLOCK), F32)
        for t in range(z.months):
            level = moved[t * z.width : (t + 1) * z.width, :] + ltv
            ahead, keep, gain = [None] * z.live, [None] * z.live, [None] * z.live
            following = [None] * z.live
            if t == 0:
                size = of_start([0.5**k for k in range(z.live)])
                roll = size * jnp.tanh(of_start(roll_base) + of_start(roll_rate) * level)
                cure = jnp.tanh(of_start(cure_base) + of_start(cure_rate) * level)
                on = size + roll
                rest = size - roll
                cured = rest * cure
                stays = rest - cured
                back = of_start([1.0] + [2.0**k for k in range(1, z.live)]) * (rest + cured)
                ahead[z.live - 1] = jnp.where(begins[z.live - 1], on, 0.0)
                for k in range(1, z.live):
                    moves = jnp.where(begins[k - 1], on, 0.0)
                    following[k] = jnp.where(begins[k], stays, moves)
                following[0] = jnp.where(begins[0], stays, back)
            else:
                for k in range(z.live):
                    if t >= z.reach(k):
                        continue
                    part = state[k] * jnp.tanh(roll_base[k] + roll_rate[k] * level)
                    ahead[k] = state[k] + part
                    if t + 1 < z.reach(k):
                        rest = state[k] - part
                        cured = rest * jnp.tanh(cure_base[k] + cure_rate[k] * level)
                        keep[k] = rest - cured
                        gain[k] = rest + cured
                for k in range(1, z.live):
                    if t + 1 < z.reach(k):
                        following[k] = ahead[k - 1] + keep[k]
                if t + 1 < z.reach(0):
                    back = gain[z.live - 1]
                    for k in range(z.live - 2, 0, -1):
                        back = 2.0 * back + gain[k]
                    following[0] = keep[0] + 2.0 * back
            severity = jnp.tanh(1.5 * level)
            scale = 0.5 * 2.0 ** (z.live - 1) * 0.25**t
            loss = loss + (0.35 * scale + (0.25 * scale) * severity) * ahead[z.live - 1]
            state = following
            if t % 4 == 3:
                d = t // 4
                high, low = pieces(balance * loss, 2)
                dated[d * z.width : (d + 1) * z.width, :] = high.astype(BF16)
                dated[marks + d * z.width : marks + (d + 1) * z.width, :] = low.astype(BF16)
        money = jnp.concatenate(balance_rows + [jnp.zeros((14, BLOCK), F32)], axis=0)
        dated[2 * marks :, :] = money.astype(BF16)
        group = j // z.sources
        sums[group] = sums[group] + lax.dot_general(
            dated[...], one_hot(j, b, 2), (((1,), (1,)), ((), ())), preferred_element_type=F32
        )

    moved = (moved_even, moved_odd)

    def source_step(j, carry):
        for b in range(z.blocks):
            fill(j, b, moved[b % 2])
        for b in range(z.blocks):
            run(j, b, moved[b % 2])
        return carry

    lax.fori_loop(0, z.devs, source_step, 0)

    for group in range(z.slot_groups):
        total = sums[group]
        money = total[2 * marks : 2 * marks + 1] + total[2 * marks + 1 : 2 * marks + 2]
        ratio = (total[0:marks] + total[marks : 2 * marks]) / money
        split = jnp.concatenate(pieces(ratio, 3), axis=0).astype(BF16)
        listed = lists[group]
        pool_id = listed[0:1] * 64.0 + listed[1:2]
        pool_iota = lax.broadcasted_iota(jnp.int32, (z.all_pools, LANES), 0).astype(F32)
        order = jnp.where(pool_iota == pool_id, 1.0, 0.0).astype(BF16)
        part = lax.dot_general(
            split, order, (((1,), (1,)), ((), ())), preferred_element_type=F32
        )
        part = part[0:marks] + part[marks : 2 * marks] + part[2 * marks :]
        ratios[...] = part if group == 0 else ratios[...] + part
    for c in range(z.chips):
        to = me ^ (2 * c)
        both = ratios[:, pl.ds(pl.multiple_of((to * z.pools // LANES) * LANES, LANES), LANES)]
        for d in range(z.dates):
            made = []
            for own in range(LANES // z.pools):
                mixed = None
                for h in range(z.halves):
                    first = d * z.width + h * z.half
                    part = rolled(both[first : first + z.half], (h - own) * z.pools)
                    mixed = part if mixed is None else jnp.where(lane // z.pools == h, part, mixed)
                made.append(mixed)
            odd = lax.rem(me, 2) == 1
            rows = slice(c * z.out_rows + d * z.half, c * z.out_rows + (d + 1) * z.half)
            kept[rows, :] = jnp.where(odd, made[1], made[0])
            passed[rows, :] = jnp.where(odd, made[0], made[1])


def owned_ratio(z, own, others, j, d):
    ref, first = part_of(z, own, others, j, z.out_rows)
    return ref[first + d * z.half : first + (d + 1) * z.half, :]


def means_kernel(z, *refs):
    own, others, (bps, out, scratch) = refs[:2], refs[2 : z.chips + 1], refs[z.chips + 1 :]
    scratch[...] = jnp.zeros_like(scratch)
    scratch[0 : z.tranches, 0 : z.pools] = bps[...].astype(F32) / 10000.0
    rows = scratch[...]
    for h in range(1, z.halves):
        rows = rows + pltpu.roll(scratch[...], h * z.pools, 1)
    out[...] = jnp.zeros_like(out)
    for d in range(z.dates):
        ratio = jnp.concatenate(
            [owned_ratio(z, own, others, j, d) for j in range(z.devs)], axis=0
        )
        for j in range(z.tranches):
            low = rows[j : j + 1]
            height = (rows[j + 1 : j + 2] if j + 1 < z.tranches else 1.0) - low
            share = jnp.clip((ratio - low) / height, 0.0, 1.0)
            out[j * z.dates + d : j * z.dates + d + 1, :] = jnp.sum(share, axis=0, keepdims=True)


def paths_kernel(z, *refs):
    own, others = refs[:2], refs[2 : z.chips + 1]
    bps, out, scratch, columns = refs[z.chips + 1 :]
    me = lax.axis_index("loan")
    columns[...] = jnp.zeros_like(columns)
    columns[0 : z.tranches, 0 : z.pools] = bps[...].astype(F32) / 10000.0
    attach = columns[...].T
    for j in range(z.devs):
        first = (me ^ j) * z.half
        scratch[pl.ds(first, z.half), :] = owned_ratio(z, own, others, j, z.dates - 1)
    turned = scratch[...].T
    ratio = jnp.concatenate(
        [turned[h * z.pools : (h + 1) * z.pools, 0 : z.side] for h in range(z.halves)], axis=1
    )
    for j in range(z.tranches):
        low = attach[0 : z.pools, j : j + 1]
        high = attach[0 : z.pools, j + 1 : j + 2] if j + 1 < z.tranches else 1.0
        out[j] = jnp.clip((ratio - low) / (high - low), 0.0, 1.0)


def total_kernel(z, left, right, out):
    total = left[...] + right[...]
    wide = total
    for h in range(1, z.halves):
        wide = wide + pltpu.roll(total, LANES - h * z.pools, 1)
    wide = wide[:, 0 : z.pools] / float(z.paths * z.path_devs)
    for j in range(z.tranches):
        out[j] = wide[j * z.dates : (j + 1) * z.dates]


def grant(mib):
    return pltpu.CompilerParams(vmem_limit_bytes=mib << 20)


def exchange(z, kept, passed, rows):
    got = lax.ppermute(passed, "loan", [(i, i ^ 1) for i in range(z.devs)])
    pairs = pl.pallas_call(
        functools.partial(pair_kernel, z, rows),
        out_shape=[jax.ShapeDtypeStruct((2 * rows, LANES), kept.dtype)] * (z.chips - 1),
        in_specs=[VMEM] * 2,
        out_specs=[VMEM] * (z.chips - 1),
        compiler_params=grant(4),
        name="pair",
    )(kept, got)
    others = [
        lax.ppermute(pairs[c - 1], "loan", [(i, i ^ (2 * c)) for i in range(z.devs)])
        for c in range(1, z.chips)
    ]
    return [kept, got] + others


def shards(
    price_moves,
    block_regions,
    region_slot,
    block_pools,
    pool_slot,
    init_state,
    balance,
    loan_to_value,
    hazard_base,
    hazard_slope,
    attach_bps,
):
    z = Sizes(price_moves, block_regions, block_pools, attach_bps, hazard_base)

    def lanes(value):
        return value.reshape(z.loan_rows, LANES)

    inputs = [
        price_moves,
        block_regions,
        block_pools,
        lanes(region_slot),
        lanes(pool_slot),
        lanes(init_state),
        lanes(balance),
        lanes(loan_to_value),
    ]
    kept, passed = pl.pallas_call(
        functools.partial(pack_kernel, z),
        out_shape=[jax.ShapeDtypeStruct((z.chips * z.rows, LANES), BF16)] * 2,
        in_specs=[pl.BlockSpec(memory_space=pltpu.HBM)] * 8,
        out_specs=[VMEM] * 2,
        scratch_shapes=[pltpu.VMEM(value.shape, value.dtype) for value in inputs]
        + [
            pltpu.VMEM((z.groups, LANES, LANES), F32),
            pltpu.VMEM((z.info_rows, LANES), F32),
            pltpu.VMEM((8, LANES), F32),
            pltpu.SemaphoreType.DMA((8,)),
        ],
        compiler_params=grant(8),
        name="pack",
    )(*[pltpu.with_memory_space_constraint(value, pltpu.HBM) for value in inputs])
    parts = exchange(z, kept, passed, z.rows)
    marks = z.dates * z.width
    moved = pltpu.VMEM((z.steps, BLOCK), F32)
    kept, passed = pl.pallas_call(
        functools.partial(months_kernel, z),
        out_shape=[jax.ShapeDtypeStruct((z.chips * z.out_rows, LANES), F32)] * 2,
        in_specs=[VMEM] * (z.chips + 1) + [SMEM] * 2,
        out_specs=[VMEM] * 2,
        scratch_shapes=[
            pltpu.VMEM((z.steps, z.devs * z.pad), BF16),
            pltpu.VMEM((z.devs, z.info_rows, LANES), F32),
            pltpu.VMEM((z.slot_groups, z.steps, 2 * LANES), BF16),
            moved,
            moved,
            pltpu.VMEM((2 * marks + 16, BLOCK), BF16),
            pltpu.VMEM((z.slot_groups, 2 * marks + 16, LANES), F32),
            pltpu.VMEM((z.slot_groups, 4, LANES), F32),
            pltpu.VMEM((marks, z.all_pools), F32),
        ],
        compiler_params=grant(16),
        name="months",
    )(*parts, hazard_base, hazard_slope)
    parts = exchange(z, kept, passed, z.out_rows)
    attach = attach_bps.T
    total_rows = -(-z.tranches * z.dates // 8) * 8
    sums = pl.pallas_call(
        functools.partial(means_kernel, z),
        out_shape=jax.ShapeDtypeStruct((total_rows, LANES), F32),
        in_specs=[VMEM] * (z.chips + 2),
        out_specs=VMEM,
        scratch_shapes=[pltpu.VMEM((8, LANES), F32)],
        compiler_params=grant(4),
        name="means",
    )(*parts, attach)
    distance = 1
    while 2 * distance < z.path_devs:
        sums = sums + lax.ppermute(sums, "path", [(i, i ^ distance) for i in range(z.path_devs)])
        distance *= 2
    other = lax.ppermute(sums, "path", [(i, i ^ distance) for i in range(z.path_devs)])
    path_loss = pl.pallas_call(
        functools.partial(paths_kernel, z),
        out_shape=jax.ShapeDtypeStruct((z.tranches, z.pools, z.paths), F32),
        in_specs=[VMEM] * (z.chips + 2),
        out_specs=VMEM,
        scratch_shapes=[pltpu.VMEM((z.side, LANES), F32), pltpu.VMEM((8, LANES), F32)],
        compiler_params=grant(4),
        name="paths",
    )(*parts, attach)
    expected_loss = pl.pallas_call(
        functools.partial(total_kernel, z),
        out_shape=jax.ShapeDtypeStruct((z.tranches, z.dates, z.pools), F32),
        in_specs=[VMEM] * 2,
        out_specs=VMEM,
        compiler_params=grant(4),
        name="total",
    )(sums, other)
    return expected_loss, path_loss


def solution(mesh):
    in_specs = (
        P(None, "loan", "path"),
        P("loan", None),
        P("loan"),
        P("loan", None),
        P("loan"),
        P("loan"),
        P("loan"),
        P("loan"),
        P(),
        P(),
        P("loan", None),
    )
    out_specs = (P(None, None, "loan"), P(None, "loan", "path"))
    return jax.shard_map(shards, mesh=mesh, in_specs=in_specs, out_specs=out_specs, check_vma=False)
```

time: 49.8 us -> 39.9 us (0.80)
  blocking collectives: 12.6 us -> 0 us
  starting transfers between devices: 7.88 us -> 13.1 us
  Pallas kernels: 18 us -> 13.5 us
  waiting for transfers between devices: 8.22 us -> 12.4 us
  local copies, waits for them, and re-layouts: 1.96 us -> 0.01 us
    all_to_all x1 -> x0, blocking collectives: 12.6 us -> none  [shards(): got = lax.all_to_all(sent, 'loan', 0, 0, tiled=True)]
    ppermute x3 -> x10, starting transfers between devices: 4.39 us -> 13.1 us  [the longest x6 8.02 us: exchange(): lax.ppermute(pairs[c - 1], 'loan', [(i, i ^ 2 * c) for i in range(z.devs)])]
    ppermute x3 -> x10, waiting for transfers between devices: 3.81 us -> 12.4 us  [the longest x6 7.34 us: exchange(): lax.ppermute(pairs[c - 1], 'loan', [(i, i ^ 2 * c) for i in range(z.devs)])]
    all_to_all x1 -> x0, waiting for transfers between devices: 4.41 us -> none  [shards(): owned = lax.all_to_all(ratios, 'loan', 0, 0, tiled=True)]
    all_to_all x1 -> x0, starting transfers between devices: 3.49 us -> none  [shards(): owned = lax.all_to_all(ratios, 'loan', 0, 0, tiled=True)]
    pallas_call x2 -> x5, Pallas kernels: 14.3 us -> 12.3 us  [the longest x1 10.4 us: shards(): pl.pallas_call(functools.partial(months_kernel, z), out_shape=[jax.ShapeD...]
    pallas_call x1, Pallas kernels: 1.81 us -> 0.18 us  [shards(): pl.pallas_call(functools.partial(means_kernel, z), out_shape=jax.ShapeDty...]
    unnamed x7 -> x6, local copies, waits for them, and re-layouts: 1.34 us -> 0.01 us
  transfers between devices with their start and end apart: 4 -> 10, of which waited for: 3 -> 10; matrix products, arithmetic and copies ran while one was open for 1% -> 0% of each run, Pallas kernels for 4% -> 3%
where the time goes in v2:
time: 39.9 us; the launch traced here: 39.8 us
  Pallas kernels  13.5 us (34%)
  starting transfers between devices  13.1 us (33%)
  waiting for transfers between devices  12.4 us (31%)
  between operations  0.68 us (2%)
    pallas_call x1, Pallas kernels, shards(): pl.pallas_call(functools.partial(months_kernel, z), out_shape=[jax.ShapeD...  10.4 us
    ppermute x6, starting transfers between devices, exchange(): lax.ppermute(pairs[c - 1], 'loan', [(i, i ^ 2 * c) for i in range(z.devs)])  8.02 us
    ppermute x6, waiting for transfers between devices, exchange(): lax.ppermute(pairs[c - 1], 'loan', [(i, i ^ 2 * c) for i in range(z.devs)])  7.34 us
    ppermute x2, starting transfers between devices, shards(): lax.ppermute(sums, 'path', [(i, i ^ distance) for i in range(z.path_devs)])  4.47 us
    ppermute x2, waiting for transfers between devices, shards(): lax.ppermute(sums, 'path', [(i, i ^ distance) for i in range(z.path_devs)])  2.87 us
    ppermute x2, waiting for transfers between devices, exchange(): got = lax.ppermute(passed, 'loan', [(i, i ^ 1) for i in range(z.devs)])  2.2 us
    pallas_call x1, Pallas kernels, shards(): pl.pallas_call(functools.partial(pack_kernel, z), out_shape=[jax.ShapeDty...  1.23 us
    pallas_call x1, Pallas kernels, shards(): pl.pallas_call(functools.partial(paths_kernel, z), out_shape=jax.ShapeDty...  1.01 us
  transfers between devices with their start and end apart: 10, of which 10 were waited for; matrix products, arithmetic and copies ran while one was open for 0% of the time, Pallas kernels for 3%

profile of v2, /device:TPU:0, one launch (start us, length us, event | category | flops | bytes accessed | tf_op | source)
XLA Modules:
  0.0 39.8 jit_solution(10700086834277724129)
XLA Ops:
  0.6 1.2 %pack.1 = (bf16[512,128]{1,0:T(8,128)(2,1)S(1)}, bf16[512,128]{1,0:T(8,128)(2,1)S(1)}) custom-call(bf16[12,52,128]{2,1,0:T(8,128)(2,1)} %refs_0_.1, s32[2,32]{1,0:T(2,128)} %refs_1_.1, s32[2,32]{1,0:T(2,128)} %refs_2_.1, s32[4,128]{1,0:T(4,128)} %bitcast.8, s32[4,128]{1,0:T(4,128)} %bitcast.9, s32[4,128]{1,0:T(4,128)} %bitcast.10, f32[4,128]{1,0:T(4,128)} %bitcast.11, ...), custom_call_target="tpu_custom_call" | custom-call | tf_op jit(solution)/shard_map/pack/pallas_call | solution.py:463
  1.9 0.6 %collective-permute-start = (bf16[512,128]{1,0:T(8,128)(2,1)S(1)}, bf16[512,128]{1,0:T(8,128)(2,1)S(1)}, u32[]{:S(2)}, u32[]{:S(2)}) collective-permute-start(bf16[512,128]{1,0:T(8,128)(2,1)S(1)} %get-tuple-element.13), channel_id=1, source_target_pairs={{0,4},{4,0},{8,12},{12,8},{16,20},{20,16},{24,28},{28,24},{1,5},{5... | collective-permute-start | bytes 393224 | tf_op jit(solution)/shard_map/ppermute | solution.py:419
  2.4 1.0 %collective-permute-done.passed.refs_1_ = bf16[512,128]{1,0:T(8,128)(2,1)S(1)} collective-permute-done((bf16[512,128]{1,0:T(8,128)(2,1)S(1)}, bf16[512,128]{1,0:T(8,128)(2,1)S(1)}, u32[]{:S(2)}, u32[]{:S(2)}) %collective-permute-start) | collective-permute-done | bytes 131104 | tf_op jit(solution)/shard_map/ppermute | solution.py:419
  3.4 2.9 %collective-permute-start.1 = (bf16[256,128]{1,0:T(8,128)(2,1)S(1)}, bf16[256,128]{1,0:T(8,128)(2,1)S(1)}, u32[]{:S(2)}, u32[]{:S(2)}) collective-permute-start(bf16[256,128]{1,0:T(8,128)(2,1)S(1)} %get-tuple-element.14), channel_id=1, source_target_pairs={{0,8},{4,12},{8,0},{12,4},{16,24},{20,28},{24,16},{28,20},{1,9},{5... | collective-permute-start | bytes 196616 | tf_op jit(solution)/shard_map/ppermute | solution.py:429
  6.3 1.5 %collective-permute-start.2 = (bf16[256,128]{1,0:T(8,128)(2,1)S(1)}, bf16[256,128]{1,0:T(8,128)(2,1)S(1)}, u32[]{:S(2)}, u32[]{:S(2)}) collective-permute-start(bf16[256,128]{1,0:T(8,128)(2,1)S(1)} %get-tuple-element.15), channel_id=1, source_target_pairs={{0,16},{4,20},{8,24},{12,28},{16,0},{20,4},{24,8},{28,12},{1,17},{... | collective-permute-start | bytes 196616 | tf_op jit(solution)/shard_map/ppermute | solution.py:429
  7.9 0.8 %collective-permute-done.1.refs_2_ = bf16[256,128]{1,0:T(8,128)(2,1)S(1)} collective-permute-done((bf16[256,128]{1,0:T(8,128)(2,1)S(1)}, bf16[256,128]{1,0:T(8,128)(2,1)S(1)}, u32[]{:S(2)}, u32[]{:S(2)}) %collective-permute-start.1) | collective-permute-done | bytes 65568 | tf_op jit(solution)/shard_map/ppermute | solution.py:429
  8.7 1.9 %collective-permute-done.2.refs_3_ = bf16[256,128]{1,0:T(8,128)(2,1)S(1)} collective-permute-done((bf16[256,128]{1,0:T(8,128)(2,1)S(1)}, bf16[256,128]{1,0:T(8,128)(2,1)S(1)}, u32[]{:S(2)}, u32[]{:S(2)}) %collective-permute-start.2) | collective-permute-done | bytes 65568 | tf_op jit(solution)/shard_map/ppermute | solution.py:429
  10.6 2.4 %collective-permute-done.3.refs_4_ = bf16[256,128]{1,0:T(8,128)(2,1)S(1)} collective-permute-done((bf16[256,128]{1,0:T(8,128)(2,1)S(1)}, bf16[256,128]{1,0:T(8,128)(2,1)S(1)}, u32[]{:S(2)}, u32[]{:S(2)}) %collective-permute-start.3) | collective-permute-done | bytes 65568 | tf_op jit(solution)/shard_map/ppermute | solution.py:429
  13.0 10.4 %months.1 = (f32[96,128]{1,0:T(8,128)S(1)}, f32[96,128]{1,0:T(8,128)S(1)}) custom-call(bf16[512,128]{1,0:T(8,128)(2,1)S(1)} %get-tuple-element.12.kept.refs_0_, bf16[512,128]{1,0:T(8,128)(2,1)S(1)} %collective-permute-done.passed.refs_1_, bf16[256,128]{1,0:T(8,128)(2,1)S(1)} %collective-permute-done.1.refs_2_, ...), custom_call_target="tpu_custom_call" | custom-call | tf_op jit(solution)/shard_map/months/pallas_call | solution.py:481
  23.5 0.1 collective-permute-start.4
  23.5 1.2 %collective-permute-done.4.passed.refs_1_ = f32[96,128]{1,0:T(8,128)S(1)} collective-permute-done((f32[96,128]{1,0:T(8,128)S(1)}, f32[96,128]{1,0:T(8,128)S(1)}, u32[]{:S(2)}, u32[]{:S(2)}) %collective-permute-start.4) | collective-permute-done | bytes 49184 | tf_op jit(solution)/shard_map/ppermute | solution.py:419
  24.8 0.6 %collective-permute-start.5 = (f32[48,128]{1,0:T(8,128)S(1)}, f32[48,128]{1,0:T(8,128)S(1)}, u32[]{:S(2)}, u32[]{:S(2)}) collective-permute-start(f32[48,128]{1,0:T(8,128)S(1)} %get-tuple-element.19), channel_id=1, source_target_pairs={{0,8},{4,12},{8,0},{12,4},{16,24},{20,28},{24,16},{28,20},{1,9},{5... | collective-permute-start | bytes 73736 | tf_op jit(solution)/shard_map/ppermute | solution.py:429
  25.4 0.5 %collective-permute-start.6 = (f32[48,128]{1,0:T(8,128)S(1)}, f32[48,128]{1,0:T(8,128)S(1)}, u32[]{:S(2)}, u32[]{:S(2)}) collective-permute-start(f32[48,128]{1,0:T(8,128)S(1)} %get-tuple-element.20), channel_id=1, source_target_pairs={{0,16},{4,20},{8,24},{12,28},{16,0},{20,4},{24,8},{28,12},{1,17},{... | collective-permute-start | bytes 73736 | tf_op jit(solution)/shard_map/ppermute | solution.py:429
  25.8 2.5 %collective-permute-start.7 = (f32[48,128]{1,0:T(8,128)S(1)}, f32[48,128]{1,0:T(8,128)S(1)}, u32[]{:S(2)}, u32[]{:S(2)}) collective-permute-start(f32[48,128]{1,0:T(8,128)S(1)} %get-tuple-element.21), channel_id=1, source_target_pairs={{0,24},{4,28},{8,16},{12,20},{16,8},{20,12},{24,0},{28,4},{1,25},{... | collective-permute-start | bytes 73736 | tf_op jit(solution)/shard_map/ppermute | solution.py:429
  28.3 0.3 collective-permute-done.5.refs_2_
  28.7 0.8 %collective-permute-done.6.refs_3_ = f32[48,128]{1,0:T(8,128)S(1)} collective-permute-done((f32[48,128]{1,0:T(8,128)S(1)}, f32[48,128]{1,0:T(8,128)S(1)}, u32[]{:S(2)}, u32[]{:S(2)}) %collective-permute-start.6) | collective-permute-done | bytes 24608 | tf_op jit(solution)/shard_map/ppermute | solution.py:429
  29.4 1.1 %collective-permute-done.7.refs_4_ = f32[48,128]{1,0:T(8,128)S(1)} collective-permute-done((f32[48,128]{1,0:T(8,128)S(1)}, f32[48,128]{1,0:T(8,128)S(1)}, u32[]{:S(2)}, u32[]{:S(2)}) %collective-permute-start.7) | collective-permute-done | bytes 24608 | tf_op jit(solution)/shard_map/ppermute | solution.py:429
  30.5 0.2 means.1
  30.7 1.7 %collective-permute-start.8 = (f32[24,128]{1,0:T(8,128)S(1)}, f32[24,128]{1,0:T(8,128)S(1)}, u32[]{:S(2)}, u32[]{:S(2)}) collective-permute-start(f32[24,128]{1,0:T(8,128)S(1)} %means.1), channel_id=1, source_target_pairs={{0,1},{1,0},{2,3},{3,2},{4,5},{5,4},{6,7},{7,6},{8,9},{9,8},{10,11... | collective-permute-start | bytes 36872 | tf_op jit(solution)/shard_map/ppermute | solution.py:514
  32.4 2.1 %collective-permute-done.8 = f32[24,128]{1,0:T(8,128)S(1)} collective-permute-done((f32[24,128]{1,0:T(8,128)S(1)}, f32[24,128]{1,0:T(8,128)S(1)}, u32[]{:S(2)}, u32[]{:S(2)}) %collective-permute-start.8) | collective-permute-done | bytes 12320 | tf_op jit(solution)/shard_map/ppermute | solution.py:514
  34.5 2.8 %collective-permute-start.9 = (f32[24,128]{1,0:T(8,128)S(1)}, f32[24,128]{1,0:T(8,128)S(1)}, u32[]{:S(2)}, u32[]{:S(2)}) collective-permute-start(f32[24,128]{1,0:T(8,128)S(1)} %add.3.left), channel_id=1, source_target_pairs={{0,2},{1,3},{2,0},{3,1},{4,6},{5,7},{6,4},{7,5},{8,10},{9,11},{10,... | collective-permute-start | bytes 36872 | tf_op jit(solution)/shard_map/ppermute | solution.py:516
  37.3 1.0 %paths.1 = f32[6,64,128]{2,1,0:T(8,128)} custom-call(f32[96,128]{1,0:T(8,128)S(1)} %get-tuple-element.17.kept.refs_0_, f32[96,128]{1,0:T(8,128)S(1)} %collective-permute-done.4.passed.refs_1_, f32[48,128]{1,0:T(8,128)S(1)} %collective-permute-done.5.refs_2_, f32[48,128]{1,0:T(8,128)S(1)} %collective-permute-done.6.refs_3_, ...), custom_call_target="tpu_custom_call" | custom-call | tf_op jit(solution)/shard_map/paths/pallas_call | solution.py:517
  38.3 0.8 %collective-permute-done.9.right = f32[24,128]{1,0:T(8,128)S(1)} collective-permute-done((f32[24,128]{1,0:T(8,128)S(1)}, f32[24,128]{1,0:T(8,128)S(1)}, u32[]{:S(2)}, u32[]{:S(2)}) %collective-permute-start.9) | collective-permute-done | bytes 12320 | tf_op jit(solution)/shard_map/ppermute | solution.py:516
  39.1 0.7 %total.1 = f32[6,3,64]{2,1,0:T(4,128)} custom-call(f32[24,128]{1,0:T(8,128)S(1)} %add.3.left, f32[24,128]{1,0:T(8,128)S(1)} %collective-permute-done.9.right), custom_call_target="tpu_custom_call" | custom-call | tf_op jit(solution)/shard_map/total/pallas_call | solution.py:526
  (10 shorter events, 0.1 us)
Async XLA Ops:
  1.9 1.5 %collective-permute-start = (bf16[512,128]{1,0:T(8,128)(2,1)S(1)}, bf16[512,128]{1,0:T(8,128)(2,1)S(1)}, u32[]{:S(2)}, u32[]{:S(2)}) collective-permute-start(bf16[512,128]{1,0:T(8,128)(2,1)S(1)} %get-tuple-element.13), channel_id=1, source_target_pairs={{0,4},{4,0},{8,12},{12,8},{16,20},{20,16},{24,28},{28,24},{1,5},{5... | collective-permute-start | bytes 393224 | tf_op jit(solution)/shard_map/ppermute | solution.py:419
  3.4 5.3 %collective-permute-start.1 = (bf16[256,128]{1,0:T(8,128)(2,1)S(1)}, bf16[256,128]{1,0:T(8,128)(2,1)S(1)}, u32[]{:S(2)}, u32[]{:S(2)}) collective-permute-start(bf16[256,128]{1,0:T(8,128)(2,1)S(1)} %get-tuple-element.14), channel_id=1, source_target_pairs={{0,8},{4,12},{8,0},{12,4},{16,24},{20,28},{24,16},{28,20},{1,9},{5... | collective-permute-start | bytes 196616 | tf_op jit(solution)/shard_map/ppermute | solution.py:429
  6.3 6.7 %copy-start.2 = (f32[2,6]{1,0:T(2,128)S(1)}, f32[2,6]{1,0:T(2,128)}, u32[]{:S(2)}) copy-start(f32[2,6]{1,0:T(2,128)} %refs_6_.1) | copy-start | bytes 148
  6.3 6.7 %copy-start.1 = (f32[2,6]{1,0:T(2,128)S(1)}, f32[2,6]{1,0:T(2,128)}, u32[]{:S(2)}) copy-start(f32[2,6]{1,0:T(2,128)} %refs_5_.1) | copy-start | bytes 148
  6.3 4.3 %collective-permute-start.2 = (bf16[256,128]{1,0:T(8,128)(2,1)S(1)}, bf16[256,128]{1,0:T(8,128)(2,1)S(1)}, u32[]{:S(2)}, u32[]{:S(2)}) collective-permute-start(bf16[256,128]{1,0:T(8,128)(2,1)S(1)} %get-tuple-element.15), channel_id=1, source_target_pairs={{0,16},{4,20},{8,24},{12,28},{16,0},{20,4},{24,8},{28,12},{1,17},{... | collective-permute-start | bytes 196616 | tf_op jit(solution)/shard_map/ppermute | solution.py:429
  7.9 5.2 %collective-permute-start.3 = (bf16[256,128]{1,0:T(8,128)(2,1)S(1)}, bf16[256,128]{1,0:T(8,128)(2,1)S(1)}, u32[]{:S(2)}, u32[]{:S(2)}) collective-permute-start(bf16[256,128]{1,0:T(8,128)(2,1)S(1)} %get-tuple-element.16), channel_id=1, source_target_pairs={{0,24},{4,28},{8,16},{12,20},{16,8},{20,12},{24,0},{28,4},{1,25},{... | collective-permute-start | bytes 196616 | tf_op jit(solution)/shard_map/ppermute | solution.py:429
  23.5 1.3 %collective-permute-start.4 = (f32[96,128]{1,0:T(8,128)S(1)}, f32[96,128]{1,0:T(8,128)S(1)}, u32[]{:S(2)}, u32[]{:S(2)}) collective-permute-start(f32[96,128]{1,0:T(8,128)S(1)} %get-tuple-element.18), channel_id=1, source_target_pairs={{0,4},{4,0},{8,12},{12,8},{16,20},{20,16},{24,28},{28,24},{1,5},{5... | collective-permute-start | bytes 147464 | tf_op jit(solution)/shard_map/ppermute | solution.py:419
  24.8 5.8 %copy-start = (s32[64,6]{0,1:T(8,128)S(1)}, s32[64,6]{0,1:T(8,128)}, u32[]{:S(2)}) copy-start(s32[64,6]{0,1:T(8,128)} %param.21) | copy-start | bytes 4612
  24.8 3.9 %collective-permute-start.5 = (f32[48,128]{1,0:T(8,128)S(1)}, f32[48,128]{1,0:T(8,128)S(1)}, u32[]{:S(2)}, u32[]{:S(2)}) collective-permute-start(f32[48,128]{1,0:T(8,128)S(1)} %get-tuple-element.19), channel_id=1, source_target_pairs={{0,8},{4,12},{8,0},{12,4},{16,24},{20,28},{24,16},{28,20},{1,9},{5... | collective-permute-start | bytes 73736 | tf_op jit(solution)/shard_map/ppermute | solution.py:429
  25.4 4.1 %collective-permute-start.6 = (f32[48,128]{1,0:T(8,128)S(1)}, f32[48,128]{1,0:T(8,128)S(1)}, u32[]{:S(2)}, u32[]{:S(2)}) collective-permute-start(f32[48,128]{1,0:T(8,128)S(1)} %get-tuple-element.20), channel_id=1, source_target_pairs={{0,16},{4,20},{8,24},{12,28},{16,0},{20,4},{24,8},{28,12},{1,17},{... | collective-permute-start | bytes 73736 | tf_op jit(solution)/shard_map/ppermute | solution.py:429
  25.8 4.7 %collective-permute-start.7 = (f32[48,128]{1,0:T(8,128)S(1)}, f32[48,128]{1,0:T(8,128)S(1)}, u32[]{:S(2)}, u32[]{:S(2)}) collective-permute-start(f32[48,128]{1,0:T(8,128)S(1)} %get-tuple-element.21), channel_id=1, source_target_pairs={{0,24},{4,28},{8,16},{12,20},{16,8},{20,12},{24,0},{28,4},{1,25},{... | collective-permute-start | bytes 73736 | tf_op jit(solution)/shard_map/ppermute | solution.py:429
  30.7 3.8 %collective-permute-start.8 = (f32[24,128]{1,0:T(8,128)S(1)}, f32[24,128]{1,0:T(8,128)S(1)}, u32[]{:S(2)}, u32[]{:S(2)}) collective-permute-start(f32[24,128]{1,0:T(8,128)S(1)} %means.1), channel_id=1, source_target_pairs={{0,1},{1,0},{2,3},{3,2},{4,5},{5,4},{6,7},{7,6},{8,9},{9,8},{10,11... | collective-permute-start | bytes 36872 | tf_op jit(solution)/shard_map/ppermute | solution.py:514
  34.5 4.6 %collective-permute-start.9 = (f32[24,128]{1,0:T(8,128)S(1)}, f32[24,128]{1,0:T(8,128)S(1)}, u32[]{:S(2)}, u32[]{:S(2)}) collective-permute-start(f32[24,128]{1,0:T(8,128)S(1)} %add.3.left), channel_id=1, source_target_pairs={{0,2},{1,3},{2,0},{3,1},{4,6},{5,7},{6,4},{7,5},{8,10},{9,11},{10,... | collective-permute-start | bytes 36872 | tf_op jit(solution)/shard_map/ppermute | solution.py:516

commit v3 on v2

--- a/solution.py
+++ b/solution.py
@@ -45,6 +45,7 @@
         self.list_row = 7 * self.loan_rows
         self.info_rows = -(-(self.list_row + 4) // 16) * 16
         self.rows = self.price_rows + self.info_rows
+        self.sent_rows = self.price_rows + self.rows
         self.dev_slots = self.blocks * self.slots
         self.sources = LANES // self.dev_slots
         self.all_pools = self.pools * self.devs
@@ -71,7 +72,7 @@
 
 
 def pack_kernel(z, *refs):
-    sources, (kept, passed), scratch = refs[:8], refs[8:10], refs[10:]
+    sources, outs, scratch = refs[:8], refs[8 : 8 + z.chips], refs[8 + z.chips :]
     moves, regions, pool_lists, region, pool, init, balance, ltv = scratch[:8]
     turned, info, table, arrived = scratch[8:]
     copies = [
@@ -95,14 +96,14 @@
                 parts.append(jnp.zeros((z.pad - z.metros, z.paths), F32))
         turned[g] = jnp.concatenate(parts, axis=0).T
     for c in range(z.chips):
-        for other, out in enumerate((kept, passed)):
+        for other in range(2):
             to = me ^ (2 * c + other)
             for g in range(z.groups):
                 both = [
                     turned[g, pl.ds(h * z.side + to * z.half, z.half), :] for h in range(z.halves)
                 ]
-                first = c * z.rows + g * z.width
-                out[first : first + z.width, :] = jnp.concatenate(both, axis=0).astype(BF16)
+                first = other * z.price_rows + g * z.width
+                outs[c][first : first + z.width, :] = jnp.concatenate(both, axis=0).astype(BF16)
     info[...] = jnp.zeros_like(info)
     values = [region[...].astype(F32), init[...].astype(F32), pool[...].astype(F32)]
     values += pieces(jnp.log(ltv[...]), 2) + pieces(balance[...], 2)
@@ -134,26 +135,21 @@
         info[z.list_row + i : z.list_row + i + 1, :] = row
     packed = info[...].astype(BF16)
     for c in range(z.chips):
-        kept[c * z.rows + z.price_rows : (c + 1) * z.rows, :] = packed
-        passed[c * z.rows + z.price_rows : (c + 1) * z.rows, :] = packed
-
-
-def pair_kernel(z, rows, kept, passed, *outs):
-    for c in range(1, z.chips):
-        outs[c - 1][0:rows, :] = kept[c * rows : (c + 1) * rows, :]
-        outs[c - 1][rows : 2 * rows, :] = passed[c * rows : (c + 1) * rows, :]
-
-
-def part_of(z, own, others, j, rows):
-    c, other = j // 2, j % 2
-    if c == 0:
-        return own[other], 0
-    return others[c - 1], other * rows
+        outs[c][2 * z.price_rows :, :] = packed
+
+
+def pass_kernel(z, rows, *refs):
+    parts, out = refs[:-1], refs[-1]
+    for c, part in enumerate(parts):
+        out[c * rows : (c + 1) * rows, :] = part[part.shape[0] - rows :, :]
 
 
 def months_kernel(z, *refs):
-    own, others = refs[:2], refs[2 : z.chips + 1]
-    base, slope, kept, passed = refs[z.chips + 1 : z.chips + 5]
+    near, (far, base, slope), outs = (
+        refs[: z.chips],
+        refs[z.chips : z.chips + 3],
+        refs[z.chips + 3 : 2 * z.chips + 3],
+    )
     (
         source_moves,
         info,
@@ -164,15 +160,20 @@
         sums,
         lists,
         ratios,
-    ) = refs[z.chips + 5 :]
+    ) = refs[2 * z.chips + 3 :]
     me = lax.axis_index("loan")
     lane = lax.broadcasted_iota(jnp.int32, (1, LANES), 1)
+
+    def prices_of(j):
+        c = j // 2
+        if j % 2 == 0:
+            return near[c][0 : z.price_rows, :]
+        return far[c * z.rows : c * z.rows + z.price_rows, :]
 
     for j in range(z.devs // z.fold):
         parts = []
         for i in range(z.fold):
-            ref, first = part_of(z, own, others, j * z.fold + i, z.rows)
-            parts.append(ref[first : first + z.price_rows, :].astype(F32))
+            parts.append(prices_of(j * z.fold + i).astype(F32))
         for h in range(z.fold):
             mixed = None
             count = min(z.groups, z.months - h * z.groups) * z.width
@@ -186,8 +187,12 @@
                 0:count
             ].astype(BF16)
     for j in range(z.devs):
-        ref, first = part_of(z, own, others, j, z.rows)
-        info[j] = ref[first + z.price_rows : first + z.rows, :].astype(F32)
+        c = j // 2
+        if j % 2 == 0:
+            part = near[c][2 * z.price_rows :, :]
+        else:
+            part = far[c * z.rows + z.price_rows : (c + 1) * z.rows, :]
+        info[j] = part.astype(F32)
     for group in range(z.slot_groups):
         total = info[group * z.sources, z.list_row : z.list_row + 4, :]
         for i in range(1, z.sources):
@@ -352,18 +357,21 @@
                     mixed = part if mixed is None else jnp.where(lane // z.pools == h, part, mixed)
                 made.append(mixed)
             odd = lax.rem(me, 2) == 1
-            rows = slice(c * z.out_rows + d * z.half, c * z.out_rows + (d + 1) * z.half)
-            kept[rows, :] = jnp.where(odd, made[1], made[0])
-            passed[rows, :] = jnp.where(odd, made[0], made[1])
-
-
-def owned_ratio(z, own, others, j, d):
-    ref, first = part_of(z, own, others, j, z.out_rows)
-    return ref[first + d * z.half : first + (d + 1) * z.half, :]
+            rows = slice(d * z.half, (d + 1) * z.half)
+            outs[c][rows, :] = jnp.where(odd, made[1], made[0])
+            rows = slice(z.out_rows + d * z.half, z.out_rows + (d + 1) * z.half)
+            outs[c][rows, :] = jnp.where(odd, made[0], made[1])
+
+
+def owned_ratio(z, near, far, j, d):
+    c = j // 2
+    if j % 2 == 0:
+        return near[c][d * z.half : (d + 1) * z.half, :]
+    return far[c * z.out_rows + d * z.half : c * z.out_rows + (d + 1) * z.half, :]
 
 
 def means_kernel(z, *refs):
-    own, others, (bps, out, scratch) = refs[:2], refs[2 : z.chips + 1], refs[z.chips + 1 :]
+    near, (far, bps, out, scratch) = refs[: z.chips], refs[z.chips :]
     scratch[...] = jnp.zeros_like(scratch)
     scratch[0 : z.tranches, 0 : z.pools] = bps[...].astype(F32) / 10000.0
     rows = scratch[...]
@@ -372,7 +380,7 @@
     out[...] = jnp.zeros_like(out)
     for d in range(z.dates):
         ratio = jnp.concatenate(
-            [owned_ratio(z, own, others, j, d) for j in range(z.devs)], axis=0
+            [owned_ratio(z, near, far, j, d) for j in range(z.devs)], axis=0
         )
         for j in range(z.tranches):
             low = rows[j : j + 1]
@@ -382,15 +390,14 @@
 
 
 def paths_kernel(z, *refs):
-    own, others = refs[:2], refs[2 : z.chips + 1]
-    bps, out, scratch, columns = refs[z.chips + 1 :]
+    near, (far, bps, out, scratch, columns) = refs[: z.chips], refs[z.chips :]
     me = lax.axis_index("loan")
     columns[...] = jnp.zeros_like(columns)
     columns[0 : z.tranches, 0 : z.pools] = bps[...].astype(F32) / 10000.0
     attach = columns[...].T
     for j in range(z.devs):
         first = (me ^ j) * z.half
-        scratch[pl.ds(first, z.half), :] = owned_ratio(z, own, others, j, z.dates - 1)
+        scratch[pl.ds(first, z.half), :] = owned_ratio(z, near, far, j, z.dates - 1)
     turned = scratch[...].T
     ratio = jnp.concatenate(
         [turned[h * z.pools : (h + 1) * z.pools, 0 : z.side] for h in range(z.halves)], axis=1
@@ -401,8 +408,11 @@
         out[j] = jnp.clip((ratio - low) / (high - low), 0.0, 1.0)
 
 
-def total_kernel(z, left, right, out):
-    total = left[...] + right[...]
+def total_kernel(z, *refs):
+    terms, out = [ref[...] for ref in refs[:-1]], refs[-1]
+    while len(terms) > 1:
+        terms = [terms[i] + terms[i + 1] for i in range(0, len(terms), 2)]
+    total = terms[0]
     wide = total
     for h in range(1, z.halves):
         wide = wide + pltpu.roll(total, LANES - h * z.pools, 1)
@@ -415,21 +425,19 @@
     return pltpu.CompilerParams(vmem_limit_bytes=mib << 20)
 
 
-def exchange(z, kept, passed, rows):
-    got = lax.ppermute(passed, "loan", [(i, i ^ 1) for i in range(z.devs)])
-    pairs = pl.pallas_call(
-        functools.partial(pair_kernel, z, rows),
-        out_shape=[jax.ShapeDtypeStruct((2 * rows, LANES), kept.dtype)] * (z.chips - 1),
-        in_specs=[VMEM] * 2,
-        out_specs=[VMEM] * (z.chips - 1),
+def exchange(z, parts, rows):
+    near = [parts[0]] + [None] * (z.chips - 1)
+    for c in range(z.chips - 1, 0, -1):
+        near[c] = lax.ppermute(parts[c], "loan", [(i, i ^ (2 * c)) for i in range(z.devs)])
+    passed = pl.pallas_call(
+        functools.partial(pass_kernel, z, rows),
+        out_shape=jax.ShapeDtypeStruct((z.chips * rows, LANES), parts[0].dtype),
+        in_specs=[VMEM] * z.chips,
+        out_specs=VMEM,
         compiler_params=grant(4),
-        name="pair",
-    )(kept, got)
-    others = [
-        lax.ppermute(pairs[c - 1], "loan", [(i, i ^ (2 * c)) for i in range(z.devs)])
-        for c in range(1, z.chips)
-    ]
-    return [kept, got] + others
+        name="pass",
+    )(*near)
+    return near + [lax.ppermute(passed, "loan", [(i, i ^ 1) for i in range(z.devs)])]
 
 
 def shards(
@@ -460,11 +468,11 @@
         lanes(balance),
         lanes(loan_to_value),
     ]
-    kept, passed = pl.pallas_call(
+    sent = pl.pallas_call(
         functools.partial(pack_kernel, z),
-        out_shape=[jax.ShapeDtypeStruct((z.chips * z.rows, LANES), BF16)] * 2,
+        out_shape=[jax.ShapeDtypeStruct((z.sent_rows, LANES), BF16)] * z.chips,
         in_specs=[pl.BlockSpec(memory_space=pltpu.HBM)] * 8,
-        out_specs=[VMEM] * 2,
+        out_specs=[VMEM] * z.chips,
         scratch_shapes=[pltpu.VMEM(value.shape, value.dtype) for value in inputs]
         + [
             pltpu.VMEM((z.groups, LANES, LANES), F32),
@@ -475,14 +483,14 @@
         compiler_params=grant(8),
         name="pack",
     )(*[pltpu.with_memory_space_constraint(value, pltpu.HBM) for value in inputs])
-    parts = exchange(z, kept, passed, z.rows)
+    parts = exchange(z, sent, z.rows)
     marks = z.dates * z.width
     moved = pltpu.VMEM((z.steps, BLOCK), F32)
-    kept, passed = pl.pallas_call(
+    sent = pl.pallas_call(
         functools.partial(months_kernel, z),
-        out_shape=[jax.ShapeDtypeStruct((z.chips * z.out_rows, LANES), F32)] * 2,
+        out_shape=[jax.ShapeDtypeStruct((2 * z.out_rows, LANES), F32)] * z.chips,
         in_specs=[VMEM] * (z.chips + 1) + [SMEM] * 2,
-        out_specs=[VMEM] * 2,
+        out_specs=[VMEM] * z.chips,
         scratch_shapes=[
             pltpu.VMEM((z.steps, z.devs * z.pad), BF16),
             pltpu.VMEM((z.devs, z.info_rows, LANES), F32),
@@ -497,7 +505,7 @@
         compiler_params=grant(16),
         name="months",
     )(*parts, hazard_base, hazard_slope)
-    parts = exchange(z, kept, passed, z.out_rows)
+    parts = exchange(z, sent, z.out_rows)
     attach = attach_bps.T
     total_rows = -(-z.tranches * z.dates // 8) * 8
     sums = pl.pallas_call(
@@ -509,11 +517,10 @@
         compiler_params=grant(4),
         name="means",
     )(*parts, attach)
-    distance = 1
-    while 2 * distance < z.path_devs:
-        sums = sums + lax.ppermute(sums, "path", [(i, i ^ distance) for i in range(z.path_devs)])
-        distance *= 2
-    other = lax.ppermute(sums, "path", [(i, i ^ distance) for i in range(z.path_devs)])
+    terms = [sums] + [
+        lax.ppermute(sums, "path", [(i, i ^ k) for i in range(z.path_devs)])
+        for k in range(1, z.path_devs)
+    ]
     path_loss = pl.pallas_call(
         functools.partial(paths_kernel, z),
         out_shape=jax.ShapeDtypeStruct((z.tranches, z.pools, z.paths), F32),
@@ -526,11 +533,11 @@
     expected_loss = pl.pallas_call(
         functools.partial(total_kernel, z),
         out_shape=jax.ShapeDtypeStruct((z.tranches, z.dates, z.pools), F32),
-        in_specs=[VMEM] * 2,
+        in_specs=[VMEM] * z.path_devs,
         out_specs=VMEM,
         compiler_params=grant(4),
         name="total",
-    )(sums, other)
+    )(*terms)
     return expected_loss, path_loss
 
 

time: 39.9 us -> 39.7 us (level)
    ppermute x10 -> x11, starting transfers between devices: 13.1 us -> 12.9 us  [the longest x6 8.13 us: exchange(): lax.ppermute(parts[c], 'loan', [(i, i ^ 2 * c) for i in range(z.devs)])]
    ppermute x10 -> x11, waiting for transfers between devices: 12.4 us -> 12.4 us  [the longest x6 6.93 us: exchange(): lax.ppermute(parts[c], 'loan', [(i, i ^ 2 * c) for i in range(z.devs)])]
  transfers between devices with their start and end apart: 10 -> 11, of which waited for: 10 -> 9; matrix products, arithmetic and copies ran while one was open for 0% -> 0% of each run, Pallas kernels for 3% -> 3%
where the time goes in v3:
time: 39.7 us; the launch traced here: 39.6 us
  Pallas kernels  13.5 us (34%)
  starting transfers between devices  12.9 us (32%)
  waiting for transfers between devices  12.4 us (31%)
  between operations  0.68 us (2%)
    pallas_call x1, Pallas kernels, shards(): pl.pallas_call(functools.partial(months_kernel, z), out_shape=[jax.ShapeD...  10.4 us
    ppermute x6, starting transfers between devices, exchange(): lax.ppermute(parts[c], 'loan', [(i, i ^ 2 * c) for i in range(z.devs)])  8.13 us
    ppermute x6, waiting for transfers between devices, exchange(): lax.ppermute(parts[c], 'loan', [(i, i ^ 2 * c) for i in range(z.devs)])  6.93 us
    ppermute x3, starting transfers between devices, shards(): lax.ppermute(sums, 'path', [(i, i ^ k) for i in range(z.path_devs)])  4.72 us
    ppermute x3, waiting for transfers between devices, shards(): lax.ppermute(sums, 'path', [(i, i ^ k) for i in range(z.path_devs)])  2.94 us
    ppermute x2, waiting for transfers between devices, exchange(): lax.ppermute(passed, 'loan', [(i, i ^ 1) for i in range(z.devs)])  2.56 us
    pallas_call x1, Pallas kernels, shards(): pl.pallas_call(functools.partial(pack_kernel, z), out_shape=[jax.ShapeDty...  1.23 us
    pallas_call x1, Pallas kernels, shards(): pl.pallas_call(functools.partial(paths_kernel, z), out_shape=jax.ShapeDty...  1.01 us
  transfers between devices with their start and end apart: 11, of which 9 were waited for; matrix products, arithmetic and copies ran while one was open for 0% of the time, Pallas kernels for 3%

profile of v3, /device:TPU:0, one launch (start us, length us, event | category | flops | bytes accessed | tf_op | source)
XLA Modules:
  0.0 39.6 jit_solution(5355787310184764044)
XLA Ops:
  0.6 1.2 %pack.1 = (bf16[224,128]{1,0:T(8,128)(2,1)S(1)}, bf16[224,128]{1,0:T(8,128)(2,1)S(1)}, bf16[224,128]{1,0:T(8,128)(2,1)S(1)}, bf16[224,128]{1,0:T(8,128)(2,1)S(1)}) custom-call(bf16[12,52,128]{2,1,0:T(8,128)(2,1)} %refs_0_.1, s32[2,32]{1,0:T(2,128)} %refs_1_.1, s32[2,32]{1,0:T(2,128)} %refs_2_.1, s32[4,128]{1,0:T(4,128)} %bitcast.8, s32[4,128]{1,0:T(4,128)} %bitcast.9, ...), custom_call_target="tpu_custom_call" | custom-call | tf_op jit(solution)/shard_map/pack/pallas_call | solution.py:471
  1.9 3.0 %collective-permute-start = (bf16[224,128]{1,0:T(8,128)(2,1)S(1)}, bf16[224,128]{1,0:T(8,128)(2,1)S(1)}, u32[]{:S(2)}, u32[]{:S(2)}) collective-permute-start(bf16[224,128]{1,0:T(8,128)(2,1)S(1)} %get-tuple-element.11), channel_id=1, source_target_pairs={{0,8},{4,12},{8,0},{12,4},{16,24},{20,28},{24,16},{28,20},{1,9},{5... | collective-permute-start | bytes 172040 | tf_op jit(solution)/shard_map/ppermute | solution.py:431
  4.9 1.5 %collective-permute-start.1 = (bf16[224,128]{1,0:T(8,128)(2,1)S(1)}, bf16[224,128]{1,0:T(8,128)(2,1)S(1)}, u32[]{:S(2)}, u32[]{:S(2)}) collective-permute-start(bf16[224,128]{1,0:T(8,128)(2,1)S(1)} %get-tuple-element.12), channel_id=1, source_target_pairs={{0,16},{4,20},{8,24},{12,28},{16,0},{20,4},{24,8},{28,12},{1,17},{... | collective-permute-start | bytes 172040 | tf_op jit(solution)/shard_map/ppermute | solution.py:431
  6.4 0.0 collective-permute-start.2
  6.4 0.6 %collective-permute-done.refs_1_ = bf16[224,128]{1,0:T(8,128)(2,1)S(1)} collective-permute-done((bf16[224,128]{1,0:T(8,128)(2,1)S(1)}, bf16[224,128]{1,0:T(8,128)(2,1)S(1)}, u32[]{:S(2)}, u32[]{:S(2)}) %collective-permute-start) | collective-permute-done | bytes 57376 | tf_op jit(solution)/shard_map/ppermute | solution.py:431
  7.1 2.0 %collective-permute-done.1.refs_2_ = bf16[224,128]{1,0:T(8,128)(2,1)S(1)} collective-permute-done((bf16[224,128]{1,0:T(8,128)(2,1)S(1)}, bf16[224,128]{1,0:T(8,128)(2,1)S(1)}, u32[]{:S(2)}, u32[]{:S(2)}) %collective-permute-start.1) | collective-permute-done | bytes 57376 | tf_op jit(solution)/shard_map/ppermute | solution.py:431
  9.1 2.4 %collective-permute-done.2.refs_3_ = bf16[224,128]{1,0:T(8,128)(2,1)S(1)} collective-permute-done((bf16[224,128]{1,0:T(8,128)(2,1)S(1)}, bf16[224,128]{1,0:T(8,128)(2,1)S(1)}, u32[]{:S(2)}, u32[]{:S(2)}) %collective-permute-start.2) | collective-permute-done | bytes 57376 | tf_op jit(solution)/shard_map/ppermute | solution.py:431
  11.5 0.1 collective-permute-start.3
  11.6 1.3 %collective-permute-done.3.refs_4_ = bf16[512,128]{1,0:T(8,128)(2,1)S(1)} collective-permute-done((bf16[512,128]{1,0:T(8,128)(2,1)S(1)}, bf16[512,128]{1,0:T(8,128)(2,1)S(1)}, u32[]{:S(2)}, u32[]{:S(2)}) %collective-permute-start.3) | collective-permute-done | bytes 131104 | tf_op jit(solution)/shard_map/ppermute | solution.py:440
  12.9 10.4 %months.1 = (f32[48,128]{1,0:T(8,128)S(1)}, f32[48,128]{1,0:T(8,128)S(1)}, f32[48,128]{1,0:T(8,128)S(1)}, f32[48,128]{1,0:T(8,128)S(1)}) custom-call(bf16[224,128]{1,0:T(8,128)(2,1)S(1)} %get-tuple-element.10.refs_0_, bf16[224,128]{1,0:T(8,128)(2,1)S(1)} %collective-permute-done.refs_1_, bf16[224,128]{1,0:T(8,128)(2,1)S(1)} %collective-permute-done.1.refs_2_, ...), custom_call_target="tpu_custom_call" | custom-call | tf_op jit(solution)/shard_map/months/pallas_call | solution.py:489
  23.4 0.6 %collective-permute-start.4 = (f32[48,128]{1,0:T(8,128)S(1)}, f32[48,128]{1,0:T(8,128)S(1)}, u32[]{:S(2)}, u32[]{:S(2)}) collective-permute-start(f32[48,128]{1,0:T(8,128)S(1)} %get-tuple-element.15), channel_id=1, source_target_pairs={{0,8},{4,12},{8,0},{12,4},{16,24},{20,28},{24,16},{28,20},{1,9},{5... | collective-permute-start | bytes 73736 | tf_op jit(solution)/shard_map/ppermute | solution.py:431
  24.0 0.1 collective-permute-start.5
  24.1 2.9 %collective-permute-start.6 = (f32[48,128]{1,0:T(8,128)S(1)}, f32[48,128]{1,0:T(8,128)S(1)}, u32[]{:S(2)}, u32[]{:S(2)}) collective-permute-start(f32[48,128]{1,0:T(8,128)S(1)} %get-tuple-element.17), channel_id=1, source_target_pairs={{0,24},{4,28},{8,16},{12,20},{16,8},{20,12},{24,0},{28,4},{1,25},{... | collective-permute-start | bytes 73736 | tf_op jit(solution)/shard_map/ppermute | solution.py:431
  26.9 0.3 collective-permute-done.4.refs_1_
  27.3 0.6 %collective-permute-done.5.refs_2_ = f32[48,128]{1,0:T(8,128)S(1)} collective-permute-done((f32[48,128]{1,0:T(8,128)S(1)}, f32[48,128]{1,0:T(8,128)S(1)}, u32[]{:S(2)}, u32[]{:S(2)}) %collective-permute-start.5) | collective-permute-done | bytes 24608 | tf_op jit(solution)/shard_map/ppermute | solution.py:431
  27.9 0.9 %collective-permute-done.6.refs_3_ = f32[48,128]{1,0:T(8,128)S(1)} collective-permute-done((f32[48,128]{1,0:T(8,128)S(1)}, f32[48,128]{1,0:T(8,128)S(1)}, u32[]{:S(2)}, u32[]{:S(2)}) %collective-permute-start.6) | collective-permute-done | bytes 24608 | tf_op jit(solution)/shard_map/ppermute | solution.py:431
  28.8 1.2 %collective-permute-done.7.refs_4_ = f32[96,128]{1,0:T(8,128)S(1)} collective-permute-done((f32[96,128]{1,0:T(8,128)S(1)}, f32[96,128]{1,0:T(8,128)S(1)}, u32[]{:S(2)}, u32[]{:S(2)}) %collective-permute-start.7) | collective-permute-done | bytes 49184 | tf_op jit(solution)/shard_map/ppermute | solution.py:440
  30.0 0.2 means.1.refs_0_
  30.2 4.1 %collective-permute-start.10 = (f32[24,128]{1,0:T(8,128)S(1)}, f32[24,128]{1,0:T(8,128)S(1)}, u32[]{:S(2)}, u32[]{:S(2)}) collective-permute-start(f32[24,128]{1,0:T(8,128)S(1)} %means.1.refs_0_), channel_id=1, source_target_pairs={{0,3},{1,2},{2,1},{3,0},{4,7},{5,6},{6,5},{7,4},{8,11},{9,10},{10,... | collective-permute-start | bytes 36872 | tf_op jit(solution)/shard_map/ppermute | solution.py:521
  34.3 0.6 %collective-permute-start.8 = (f32[24,128]{1,0:T(8,128)S(1)}, f32[24,128]{1,0:T(8,128)S(1)}, u32[]{:S(2)}, u32[]{:S(2)}) collective-permute-start(f32[24,128]{1,0:T(8,128)S(1)} %means.1.refs_0_), channel_id=1, source_target_pairs={{0,1},{1,0},{2,3},{3,2},{4,5},{5,4},{6,7},{7,6},{8,9},{9,8},{10,11... | collective-permute-start | bytes 36872 | tf_op jit(solution)/shard_map/ppermute | solution.py:521
  34.9 1.0 %paths.1 = f32[6,64,128]{2,1,0:T(8,128)} custom-call(f32[48,128]{1,0:T(8,128)S(1)} %get-tuple-element.14.refs_0_, f32[48,128]{1,0:T(8,128)S(1)} %collective-permute-done.4.refs_1_, f32[48,128]{1,0:T(8,128)S(1)} %collective-permute-done.5.refs_2_, f32[48,128]{1,0:T(8,128)S(1)} %collective-permute-done.6.refs_3_, ...), custom_call_target="tpu_custom_call" | custom-call | tf_op jit(solution)/shard_map/paths/pallas_call | solution.py:524
  35.9 0.0 collective-permute-done.10.refs_3_
  36.0 2.9 %collective-permute-done.9.refs_2_ = f32[24,128]{1,0:T(8,128)S(1)} collective-permute-done((f32[24,128]{1,0:T(8,128)S(1)}, f32[24,128]{1,0:T(8,128)S(1)}, u32[]{:S(2)}, u32[]{:S(2)}) %collective-permute-start.9) | collective-permute-done | bytes 12320 | tf_op jit(solution)/shard_map/ppermute | solution.py:521
  38.9 0.7 %total.1 = f32[6,3,64]{2,1,0:T(4,128)} custom-call(f32[24,128]{1,0:T(8,128)S(1)} %means.1.refs_0_, f32[24,128]{1,0:T(8,128)S(1)} %collective-permute-done.8.refs_1_, f32[24,128]{1,0:T(8,128)S(1)} %collective-permute-done.9.refs_2_, f32[24,128]{1,0:T(8,128)S(1)} %collective-permute-done.10.refs_3_), custom_call_target="tpu_custom_call" | custom-call | tf_op jit(solution)/shard_map/total/pallas_call | solution.py:533
  (11 shorter events, 0.0 us)
Async XLA Ops:
  1.9 5.2 %collective-permute-start = (bf16[224,128]{1,0:T(8,128)(2,1)S(1)}, bf16[224,128]{1,0:T(8,128)(2,1)S(1)}, u32[]{:S(2)}, u32[]{:S(2)}) collective-permute-start(bf16[224,128]{1,0:T(8,128)(2,1)S(1)} %get-tuple-element.11), channel_id=1, source_target_pairs={{0,8},{4,12},{8,0},{12,4},{16,24},{20,28},{24,16},{28,20},{1,9},{5... | collective-permute-start | bytes 172040 | tf_op jit(solution)/shard_map/ppermute | solution.py:431
  4.9 4.2 %collective-permute-start.1 = (bf16[224,128]{1,0:T(8,128)(2,1)S(1)}, bf16[224,128]{1,0:T(8,128)(2,1)S(1)}, u32[]{:S(2)}, u32[]{:S(2)}) collective-permute-start(bf16[224,128]{1,0:T(8,128)(2,1)S(1)} %get-tuple-element.12), channel_id=1, source_target_pairs={{0,16},{4,20},{8,24},{12,28},{16,0},{20,4},{24,8},{28,12},{1,17},{... | collective-permute-start | bytes 172040 | tf_op jit(solution)/shard_map/ppermute | solution.py:431
  6.4 5.1 %collective-permute-start.2 = (bf16[224,128]{1,0:T(8,128)(2,1)S(1)}, bf16[224,128]{1,0:T(8,128)(2,1)S(1)}, u32[]{:S(2)}, u32[]{:S(2)}) collective-permute-start(bf16[224,128]{1,0:T(8,128)(2,1)S(1)} %get-tuple-element.13), channel_id=1, source_target_pairs={{0,24},{4,28},{8,16},{12,20},{16,8},{20,12},{24,0},{28,4},{1,25},{... | collective-permute-start | bytes 172040 | tf_op jit(solution)/shard_map/ppermute | solution.py:431
  11.5 1.4 %copy-start.1 = (f32[2,6]{1,0:T(2,128)S(1)}, f32[2,6]{1,0:T(2,128)}, u32[]{:S(2)}) copy-start(f32[2,6]{1,0:T(2,128)} %refs_5_.1) | copy-start | bytes 148
  11.5 1.4 %copy-start.2 = (f32[2,6]{1,0:T(2,128)S(1)}, f32[2,6]{1,0:T(2,128)}, u32[]{:S(2)}) copy-start(f32[2,6]{1,0:T(2,128)} %refs_6_.1) | copy-start | bytes 148
  11.5 1.4 %collective-permute-start.3 = (bf16[512,128]{1,0:T(8,128)(2,1)S(1)}, bf16[512,128]{1,0:T(8,128)(2,1)S(1)}, u32[]{:S(2)}, u32[]{:S(2)}) collective-permute-start(bf16[512,128]{1,0:T(8,128)(2,1)S(1)} %pass.2), channel_id=1, source_target_pairs={{0,4},{4,0},{8,12},{12,8},{16,20},{20,16},{24,28},{28,24},{1,5},{5... | collective-permute-start | bytes 393224 | tf_op jit(solution)/shard_map/ppermute | solution.py:440
  23.4 3.9 %collective-permute-start.4 = (f32[48,128]{1,0:T(8,128)S(1)}, f32[48,128]{1,0:T(8,128)S(1)}, u32[]{:S(2)}, u32[]{:S(2)}) collective-permute-start(f32[48,128]{1,0:T(8,128)S(1)} %get-tuple-element.15), channel_id=1, source_target_pairs={{0,8},{4,12},{8,0},{12,4},{16,24},{20,28},{24,16},{28,20},{1,9},{5... | collective-permute-start | bytes 73736 | tf_op jit(solution)/shard_map/ppermute | solution.py:431
  24.0 3.9 %collective-permute-start.5 = (f32[48,128]{1,0:T(8,128)S(1)}, f32[48,128]{1,0:T(8,128)S(1)}, u32[]{:S(2)}, u32[]{:S(2)}) collective-permute-start(f32[48,128]{1,0:T(8,128)S(1)} %get-tuple-element.16), channel_id=1, source_target_pairs={{0,16},{4,20},{8,24},{12,28},{16,0},{20,4},{24,8},{28,12},{1,17},{... | collective-permute-start | bytes 73736 | tf_op jit(solution)/shard_map/ppermute | solution.py:431
  24.1 4.7 %collective-permute-start.6 = (f32[48,128]{1,0:T(8,128)S(1)}, f32[48,128]{1,0:T(8,128)S(1)}, u32[]{:S(2)}, u32[]{:S(2)}) collective-permute-start(f32[48,128]{1,0:T(8,128)S(1)} %get-tuple-element.17), channel_id=1, source_target_pairs={{0,24},{4,28},{8,16},{12,20},{16,8},{20,12},{24,0},{28,4},{1,25},{... | collective-permute-start | bytes 73736 | tf_op jit(solution)/shard_map/ppermute | solution.py:431
  28.8 1.2 %copy-start = (s32[64,6]{0,1:T(8,128)S(1)}, s32[64,6]{0,1:T(8,128)}, u32[]{:S(2)}) copy-start(s32[64,6]{0,1:T(8,128)} %param.21) | copy-start | bytes 4612
  28.8 1.2 %collective-permute-start.7 = (f32[96,128]{1,0:T(8,128)S(1)}, f32[96,128]{1,0:T(8,128)S(1)}, u32[]{:S(2)}, u32[]{:S(2)}) collective-permute-start(f32[96,128]{1,0:T(8,128)S(1)} %pass.3), channel_id=1, source_target_pairs={{0,4},{4,0},{8,12},{12,8},{16,20},{20,16},{24,28},{28,24},{1,5},{5... | collective-permute-start | bytes 147464 | tf_op jit(solution)/shard_map/ppermute | solution.py:440
  30.2 5.7 %collective-permute-start.10 = (f32[24,128]{1,0:T(8,128)S(1)}, f32[24,128]{1,0:T(8,128)S(1)}, u32[]{:S(2)}, u32[]{:S(2)}) collective-permute-start(f32[24,128]{1,0:T(8,128)S(1)} %means.1.refs_0_), channel_id=1, source_target_pairs={{0,3},{1,2},{2,1},{3,0},{4,7},{5,6},{6,5},{7,4},{8,11},{9,10},{10,... | collective-permute-start | bytes 36872 | tf_op jit(solution)/shard_map/ppermute | solution.py:521
  34.3 4.6 %collective-permute-start.9 = (f32[24,128]{1,0:T(8,128)S(1)}, f32[24,128]{1,0:T(8,128)S(1)}, u32[]{:S(2)}, u32[]{:S(2)}) collective-permute-start(f32[24,128]{1,0:T(8,128)S(1)} %means.1.refs_0_), channel_id=1, source_target_pairs={{0,2},{1,3},{2,0},{3,1},{4,6},{5,7},{6,4},{7,5},{8,10},{9,11},{10,... | collective-permute-start | bytes 36872 | tf_op jit(solution)/shard_map/ppermute | solution.py:521
  34.3 4.6 %collective-permute-start.8 = (f32[24,128]{1,0:T(8,128)S(1)}, f32[24,128]{1,0:T(8,128)S(1)}, u32[]{:S(2)}, u32[]{:S(2)}) collective-permute-start(f32[24,128]{1,0:T(8,128)S(1)} %means.1.refs_0_), channel_id=1, source_target_pairs={{0,1},{1,0},{2,3},{3,2},{4,5},{5,4},{6,7},{7,6},{8,9},{9,8},{10,11... | collective-permute-start | bytes 36872 | tf_op jit(solution)/shard_map/ppermute | solution.py:521

commit v4 on v3

--- a/solution.py
+++ b/solution.py
@@ -153,6 +153,7 @@
     (
         source_moves,
         info,
+        loans,
         both_pieces,
         moved_even,
         moved_odd,
@@ -216,25 +217,50 @@
         chooser = jnp.where(key_row == key, 1.0, 0.0).astype(BF16)
         moved = jnp.dot(source_moves[...], chooser, preferred_element_type=F32)
         level = jnp.zeros((z.width, LANES), F32)
-        highs, lows = [], []
+        levels = []
         for t in range(z.months):
             level = level + (stress - moved[t * z.width : (t + 1) * z.width])
-            high, low = pieces(level, 2)
-            highs.append(high)
-            lows.append(low)
-        both_pieces[group, :, 0:LANES] = jnp.concatenate(highs, axis=0).astype(BF16)
-        both_pieces[group, :, LANES:] = jnp.concatenate(lows, axis=0).astype(BF16)
-    roll_base = [0.5 * base[0, k] for k in range(z.live)]
-    roll_rate = [0.5 * slope[0, k] for k in range(z.live)]
-    cure_base = [0.5 * base[1, k] for k in range(z.live)]
-    cure_rate = [-0.5 * slope[1, k] for k in range(z.live)]
+            levels.append(level)
+        level = jnp.concatenate(levels, axis=0)
+        high, low = pieces((0.5 * slope[0, z.live - 1]) * level, 2)
+        both_pieces[group, :, 0:LANES] = high.astype(BF16)
+        both_pieces[group, :, LANES:] = low.astype(BF16)
+    last_base, last_rate = 0.5 * base[0, z.live - 1], 0.5 * slope[0, z.live - 1]
+    roll_rate = [slope[0, k] / slope[0, z.live - 1] for k in range(z.live)]
+    cure_rate = [-(slope[1, k] / slope[0, z.live - 1]) for k in range(z.live)]
+    roll_base = [0.5 * base[0, k] - roll_rate[k] * last_base for k in range(z.live)]
+    cure_base = [0.5 * base[1, k] - cure_rate[k] * last_base for k in range(z.live)]
+    severity_rate = 3.0 / slope[0, z.live - 1]
+    severity_base = -(severity_rate * last_base)
+    for j in range(z.devs):
+        rows = [info[j, q * z.loan_rows : (q + 1) * z.loan_rows, :] for q in range(7)]
+        ltv = rows[3] + rows[4]
+
+        def of_start(values):
+            chosen = jnp.full(rows[1].shape, values[0], F32)
+            for k in range(1, z.live):
+                chosen = jnp.where(rows[1] == float(k), values[k], chosen)
+            return chosen
+
+        per_loan = [
+            last_base + last_rate * ltv,
+            rows[5] + rows[6],
+            of_start([0.5**k for k in range(z.live)]),
+            of_start([2.0**k for k in range(z.live)]),
+        ]
+        for rates in (roll_base, roll_rate, cure_base, cure_rate):
+            per_loan.append(of_start(rates))
+        for rates in (roll_base, roll_rate, cure_base, cure_rate):
+            per_loan.append(of_start(rates[1:] + [0.0]))
+        for q, value in enumerate(per_loan):
+            loans[j, q * z.loan_rows : (q + 1) * z.loan_rows, :] = value
     sums[...] = jnp.zeros_like(sums)
     marks = z.dates * z.width
     slot_row = lax.broadcasted_iota(jnp.int32, (z.regions, BLOCK), 0).astype(F32)
 
-    def row(j, b, q):
+    def row(j, b, q, values=info):
         first = q * z.loan_rows + b * z.per
-        both = info[j, first : first + z.per, :]
+        both = values[j, first : first + z.per, :]
         return jnp.concatenate([both[r : r + 1, :] for r in range(z.per)], axis=1)
 
     def one_hot(j, b, q):
@@ -254,58 +280,71 @@
     def run(j, b, moved):
         start = row(j, b, 1)
         begins = [start == float(k) for k in range(z.live)]
-        ltv = row(j, b, 3) + row(j, b, 4)
         balance_rows = [row(j, b, q) for q in (5, 6)]
-        balance = balance_rows[0] + balance_rows[1]
-
-        def of_start(values):
-            chosen = jnp.full((1, BLOCK), values[0], F32)
-            for k in range(1, z.live):
-                chosen = jnp.where(begins[k], values[k], chosen)
-            return chosen
+        own_last, balance, size, power = [row(j, b, q, loans) for q in range(4)]
+        rates = [row(j, b, q, loans) for q in range(4, 12)]
+        top = z.live - 1
+
+        def step(mass, roll_offset, roll_rate, cure_offset, cure_rate, x):
+            part = mass * jnp.tanh(roll_offset + roll_rate * x)
+            rest = mass - part
+            cured = rest * jnp.tanh(cure_offset + cure_rate * x)
+            return mass + part, rest - cured, rest + cured
 
         state = None
         loss = jnp.zeros((z.width, BLOCK), F32)
         for t in range(z.months):
-            level = moved[t * z.width : (t + 1) * z.width, :] + ltv
+            x = moved[t * z.width : (t + 1) * z.width, :] + own_last
             ahead, keep, gain = [None] * z.live, [None] * z.live, [None] * z.live
             following = [None] * z.live
             if t == 0:
-                size = of_start([0.5**k for k in range(z.live)])
-                roll = size * jnp.tanh(of_start(roll_base) + of_start(roll_rate) * level)
-                cure = jnp.tanh(of_start(cure_base) + of_start(cure_rate) * level)
-                on = size + roll
-                rest = size - roll
-                cured = rest * cure
-                stays = rest - cured
-                back = of_start([1.0] + [2.0**k for k in range(1, z.live)]) * (rest + cured)
-                ahead[z.live - 1] = jnp.where(begins[z.live - 1], on, 0.0)
+                on, stays, back = step(size, *rates[:4], x)
+                ahead[top] = jnp.where(begins[top], on, 0.0)
+                following = [
+                    stays,
+                    jnp.where(begins[top], 0.0, on),
+                    jnp.where(begins[0], 0.0, power * back),
+                ]
+            elif t == 1:
+                on, stays, back = step(state[0], *rates[:4], x)
+                next_on, next_stays, next_back = step(state[1], *rates[4:], x)
+                first_on, first_stays, _ = step(
+                    state[2], roll_base[0], roll_rate[0], cure_base[0], cure_rate[0], x
+                )
+                middle = on + next_stays
+                ahead[top] = jnp.where(
+                    begins[top], on, jnp.where(begins[top - 1], next_on, 0.0)
+                )
                 for k in range(1, z.live):
-                    moves = jnp.where(begins[k - 1], on, 0.0)
-                    following[k] = jnp.where(begins[k], stays, moves)
-                following[0] = jnp.where(begins[0], stays, back)
+                    value = jnp.where(begins[k - 2], next_on, 0.0) if k > 1 else 0.0
+                    value = jnp.where(begins[k - 1], middle, value)
+                    following[k] = jnp.where(begins[k], stays, value)
+                following[1] = following[1] + first_on
+                own = jnp.where(begins[0], stays, power * back)
+                following[0] = own + (2.0 * power) * next_back + first_stays
             else:
                 for k in range(z.live):
                     if t >= z.reach(k):
                         continue
-                    part = state[k] * jnp.tanh(roll_base[k] + roll_rate[k] * level)
+                    argument = x if k == top else roll_base[k] + roll_rate[k] * x
+                    part = state[k] * jnp.tanh(argument)
                     ahead[k] = state[k] + part
                     if t + 1 < z.reach(k):
                         rest = state[k] - part
-                        cured = rest * jnp.tanh(cure_base[k] + cure_rate[k] * level)
+                        cured = rest * jnp.tanh(cure_base[k] + cure_rate[k] * x)
                         keep[k] = rest - cured
                         gain[k] = rest + cured
                 for k in range(1, z.live):
                     if t + 1 < z.reach(k):
                         following[k] = ahead[k - 1] + keep[k]
                 if t + 1 < z.reach(0):
-                    back = gain[z.live - 1]
-                    for k in range(z.live - 2, 0, -1):
+                    back = gain[top]
+                    for k in range(top - 1, 0, -1):
                         back = 2.0 * back + gain[k]
                     following[0] = keep[0] + 2.0 * back
-            severity = jnp.tanh(1.5 * level)
+            severity = jnp.tanh(severity_base + severity_rate * x)
             scale = 0.5 * 2.0 ** (z.live - 1) * 0.25**t
-            loss = loss + (0.35 * scale + (0.25 * scale) * severity) * ahead[z.live - 1]
+            loss = loss + (0.35 * scale + (0.25 * scale) * severity) * ahead[top]
             state = following
             if t % 4 == 3:
                 d = t // 4
@@ -321,14 +360,18 @@
 
     moved = (moved_even, moved_odd)
 
-    def source_step(j, carry):
-        for b in range(z.blocks):
-            fill(j, b, moved[b % 2])
-        for b in range(z.blocks):
-            run(j, b, moved[b % 2])
+    unroll = min(8, z.devs)
+
+    def source_step(step, carry):
+        order = [(step * unroll + i, b) for i in range(unroll) for b in range(z.blocks)]
+        fill(*order[0], moved[0])
+        for i, (j, b) in enumerate(order):
+            if i + 1 < len(order):
+                fill(*order[i + 1], moved[(i + 1) % 2])
+            run(j, b, moved[i % 2])
         return carry
 
-    lax.fori_loop(0, z.devs, source_step, 0)
+    lax.fori_loop(0, z.devs // unroll, source_step, 0)
 
     for group in range(z.slot_groups):
         total = sums[group]
@@ -494,6 +537,7 @@
         scratch_shapes=[
             pltpu.VMEM((z.steps, z.devs * z.pad), BF16),
             pltpu.VMEM((z.devs, z.info_rows, LANES), F32),
+            pltpu.VMEM((z.devs, 12 * z.loan_rows, LANES), F32),
             pltpu.VMEM((z.slot_groups, z.steps, 2 * LANES), BF16),
             moved,
             moved,

time: 39.7 us -> 37.4 us (0.942)
  Pallas kernels: 13.5 us -> 11.2 us
    pallas_call x1, Pallas kernels: 10.4 us -> 8.12 us  [shards(): pl.pallas_call(functools.partial(months_kernel, z), out_shape=[jax.ShapeD...]
where the time goes in v4:
time: 37.4 us; the launch traced here: 37.3 us
  starting transfers between devices  12.9 us (34%)
  waiting for transfers between devices  12.4 us (33%)
  Pallas kernels  11.2 us (30%)
  between operations  0.68 us (2%)
    ppermute x6, starting transfers between devices, exchange(): lax.ppermute(parts[c], 'loan', [(i, i ^ 2 * c) for i in range(z.devs)])  8.13 us
    pallas_call x1, Pallas kernels, shards(): pl.pallas_call(functools.partial(months_kernel, z), out_shape=[jax.ShapeD...  8.12 us
    ppermute x6, waiting for transfers between devices, exchange(): lax.ppermute(parts[c], 'loan', [(i, i ^ 2 * c) for i in range(z.devs)])  6.94 us
    ppermute x3, starting transfers between devices, shards(): lax.ppermute(sums, 'path', [(i, i ^ k) for i in range(z.path_devs)])  4.71 us
    ppermute x3, waiting for transfers between devices, shards(): lax.ppermute(sums, 'path', [(i, i ^ k) for i in range(z.path_devs)])  2.94 us
    ppermute x2, waiting for transfers between devices, exchange(): lax.ppermute(passed, 'loan', [(i, i ^ 1) for i in range(z.devs)])  2.56 us
    pallas_call x1, Pallas kernels, shards(): pl.pallas_call(functools.partial(pack_kernel, z), out_shape=[jax.ShapeDty...  1.23 us
    pallas_call x1, Pallas kernels, shards(): pl.pallas_call(functools.partial(paths_kernel, z), out_shape=jax.ShapeDty...  1.01 us
  transfers between devices with their start and end apart: 11, of which 9 were waited for; matrix products, arithmetic and copies ran while one was open for 0% of the time, Pallas kernels for 3%

profile of v4, /device:TPU:0, one launch (start us, length us, event | category | flops | bytes accessed | tf_op | source)
XLA Modules:
  0.0 37.3 jit_solution(15060290819811518931)
XLA Ops:
  0.6 1.2 %pack.1 = (bf16[224,128]{1,0:T(8,128)(2,1)S(1)}, bf16[224,128]{1,0:T(8,128)(2,1)S(1)}, bf16[224,128]{1,0:T(8,128)(2,1)S(1)}, bf16[224,128]{1,0:T(8,128)(2,1)S(1)}) custom-call(bf16[12,52,128]{2,1,0:T(8,128)(2,1)} %refs_0_.1, s32[2,32]{1,0:T(2,128)} %refs_1_.1, s32[2,32]{1,0:T(2,128)} %refs_2_.1, s32[4,128]{1,0:T(4,128)} %bitcast.8, s32[4,128]{1,0:T(4,128)} %bitcast.9, ...), custom_call_target="tpu_custom_call" | custom-call | tf_op jit(solution)/shard_map/pack/pallas_call | solution.py:514
  1.9 3.0 %collective-permute-start = (bf16[224,128]{1,0:T(8,128)(2,1)S(1)}, bf16[224,128]{1,0:T(8,128)(2,1)S(1)}, u32[]{:S(2)}, u32[]{:S(2)}) collective-permute-start(bf16[224,128]{1,0:T(8,128)(2,1)S(1)} %get-tuple-element.11), channel_id=1, source_target_pairs={{0,8},{4,12},{8,0},{12,4},{16,24},{20,28},{24,16},{28,20},{1,9},{5... | collective-permute-start | bytes 172040 | tf_op jit(solution)/shard_map/ppermute | solution.py:474
  4.9 1.5 %collective-permute-start.1 = (bf16[224,128]{1,0:T(8,128)(2,1)S(1)}, bf16[224,128]{1,0:T(8,128)(2,1)S(1)}, u32[]{:S(2)}, u32[]{:S(2)}) collective-permute-start(bf16[224,128]{1,0:T(8,128)(2,1)S(1)} %get-tuple-element.12), channel_id=1, source_target_pairs={{0,16},{4,20},{8,24},{12,28},{16,0},{20,4},{24,8},{28,12},{1,17},{... | collective-permute-start | bytes 172040 | tf_op jit(solution)/shard_map/ppermute | solution.py:474
  6.4 0.0 collective-permute-start.2
  6.4 0.6 %collective-permute-done.refs_1_ = bf16[224,128]{1,0:T(8,128)(2,1)S(1)} collective-permute-done((bf16[224,128]{1,0:T(8,128)(2,1)S(1)}, bf16[224,128]{1,0:T(8,128)(2,1)S(1)}, u32[]{:S(2)}, u32[]{:S(2)}) %collective-permute-start) | collective-permute-done | bytes 57376 | tf_op jit(solution)/shard_map/ppermute | solution.py:474
  7.1 2.0 %collective-permute-done.1.refs_2_ = bf16[224,128]{1,0:T(8,128)(2,1)S(1)} collective-permute-done((bf16[224,128]{1,0:T(8,128)(2,1)S(1)}, bf16[224,128]{1,0:T(8,128)(2,1)S(1)}, u32[]{:S(2)}, u32[]{:S(2)}) %collective-permute-start.1) | collective-permute-done | bytes 57376 | tf_op jit(solution)/shard_map/ppermute | solution.py:474
  9.1 2.4 %collective-permute-done.2.refs_3_ = bf16[224,128]{1,0:T(8,128)(2,1)S(1)} collective-permute-done((bf16[224,128]{1,0:T(8,128)(2,1)S(1)}, bf16[224,128]{1,0:T(8,128)(2,1)S(1)}, u32[]{:S(2)}, u32[]{:S(2)}) %collective-permute-start.2) | collective-permute-done | bytes 57376 | tf_op jit(solution)/shard_map/ppermute | solution.py:474
  11.5 0.1 collective-permute-start.3
  11.6 1.3 %collective-permute-done.3.refs_4_ = bf16[512,128]{1,0:T(8,128)(2,1)S(1)} collective-permute-done((bf16[512,128]{1,0:T(8,128)(2,1)S(1)}, bf16[512,128]{1,0:T(8,128)(2,1)S(1)}, u32[]{:S(2)}, u32[]{:S(2)}) %collective-permute-start.3) | collective-permute-done | bytes 131104 | tf_op jit(solution)/shard_map/ppermute | solution.py:483
  12.9 8.1 %months.1 = (f32[48,128]{1,0:T(8,128)S(1)}, f32[48,128]{1,0:T(8,128)S(1)}, f32[48,128]{1,0:T(8,128)S(1)}, f32[48,128]{1,0:T(8,128)S(1)}) custom-call(bf16[224,128]{1,0:T(8,128)(2,1)S(1)} %get-tuple-element.10.refs_0_, bf16[224,128]{1,0:T(8,128)(2,1)S(1)} %collective-permute-done.refs_1_, bf16[224,128]{1,0:T(8,128)(2,1)S(1)} %collective-permute-done.1.refs_2_, ...), custom_call_target="tpu_custom_call" | custom-call | tf_op jit(solution)/shard_map/months/pallas_call | solution.py:532
  21.1 0.6 %collective-permute-start.4 = (f32[48,128]{1,0:T(8,128)S(1)}, f32[48,128]{1,0:T(8,128)S(1)}, u32[]{:S(2)}, u32[]{:S(2)}) collective-permute-start(f32[48,128]{1,0:T(8,128)S(1)} %get-tuple-element.15), channel_id=1, source_target_pairs={{0,8},{4,12},{8,0},{12,4},{16,24},{20,28},{24,16},{28,20},{1,9},{5... | collective-permute-start | bytes 73736 | tf_op jit(solution)/shard_map/ppermute | solution.py:474
  21.7 0.1 collective-permute-start.5
  21.8 2.8 %collective-permute-start.6 = (f32[48,128]{1,0:T(8,128)S(1)}, f32[48,128]{1,0:T(8,128)S(1)}, u32[]{:S(2)}, u32[]{:S(2)}) collective-permute-start(f32[48,128]{1,0:T(8,128)S(1)} %get-tuple-element.17), channel_id=1, source_target_pairs={{0,24},{4,28},{8,16},{12,20},{16,8},{20,12},{24,0},{28,4},{1,25},{... | collective-permute-start | bytes 73736 | tf_op jit(solution)/shard_map/ppermute | solution.py:474
  24.6 0.3 collective-permute-done.4.refs_1_
  25.0 0.6 %collective-permute-done.5.refs_2_ = f32[48,128]{1,0:T(8,128)S(1)} collective-permute-done((f32[48,128]{1,0:T(8,128)S(1)}, f32[48,128]{1,0:T(8,128)S(1)}, u32[]{:S(2)}, u32[]{:S(2)}) %collective-permute-start.5) | collective-permute-done | bytes 24608 | tf_op jit(solution)/shard_map/ppermute | solution.py:474
  25.6 0.9 %collective-permute-done.6.refs_3_ = f32[48,128]{1,0:T(8,128)S(1)} collective-permute-done((f32[48,128]{1,0:T(8,128)S(1)}, f32[48,128]{1,0:T(8,128)S(1)}, u32[]{:S(2)}, u32[]{:S(2)}) %collective-permute-start.6) | collective-permute-done | bytes 24608 | tf_op jit(solution)/shard_map/ppermute | solution.py:474
  26.5 1.2 %collective-permute-done.7.refs_4_ = f32[96,128]{1,0:T(8,128)S(1)} collective-permute-done((f32[96,128]{1,0:T(8,128)S(1)}, f32[96,128]{1,0:T(8,128)S(1)}, u32[]{:S(2)}, u32[]{:S(2)}) %collective-permute-start.7) | collective-permute-done | bytes 49184 | tf_op jit(solution)/shard_map/ppermute | solution.py:483
  27.7 0.2 means.1.refs_0_
  27.9 4.1 %collective-permute-start.10 = (f32[24,128]{1,0:T(8,128)S(1)}, f32[24,128]{1,0:T(8,128)S(1)}, u32[]{:S(2)}, u32[]{:S(2)}) collective-permute-start(f32[24,128]{1,0:T(8,128)S(1)} %means.1.refs_0_), channel_id=1, source_target_pairs={{0,3},{1,2},{2,1},{3,0},{4,7},{5,6},{6,5},{7,4},{8,11},{9,10},{10,... | collective-permute-start | bytes 36872 | tf_op jit(solution)/shard_map/ppermute | solution.py:565
  32.0 0.6 %collective-permute-start.8 = (f32[24,128]{1,0:T(8,128)S(1)}, f32[24,128]{1,0:T(8,128)S(1)}, u32[]{:S(2)}, u32[]{:S(2)}) collective-permute-start(f32[24,128]{1,0:T(8,128)S(1)} %means.1.refs_0_), channel_id=1, source_target_pairs={{0,1},{1,0},{2,3},{3,2},{4,5},{5,4},{6,7},{7,6},{8,9},{9,8},{10,11... | collective-permute-start | bytes 36872 | tf_op jit(solution)/shard_map/ppermute | solution.py:565
  32.6 1.0 %paths.1 = f32[6,64,128]{2,1,0:T(8,128)} custom-call(f32[48,128]{1,0:T(8,128)S(1)} %get-tuple-element.14.refs_0_, f32[48,128]{1,0:T(8,128)S(1)} %collective-permute-done.4.refs_1_, f32[48,128]{1,0:T(8,128)S(1)} %collective-permute-done.5.refs_2_, f32[48,128]{1,0:T(8,128)S(1)} %collective-permute-done.6.refs_3_, ...), custom_call_target="tpu_custom_call" | custom-call | tf_op jit(solution)/shard_map/paths/pallas_call | solution.py:568
  33.6 0.0 collective-permute-done.10.refs_3_
  33.7 2.9 %collective-permute-done.9.refs_2_ = f32[24,128]{1,0:T(8,128)S(1)} collective-permute-done((f32[24,128]{1,0:T(8,128)S(1)}, f32[24,128]{1,0:T(8,128)S(1)}, u32[]{:S(2)}, u32[]{:S(2)}) %collective-permute-start.9) | collective-permute-done | bytes 12320 | tf_op jit(solution)/shard_map/ppermute | solution.py:565
  36.6 0.7 %total.1 = f32[6,3,64]{2,1,0:T(4,128)} custom-call(f32[24,128]{1,0:T(8,128)S(1)} %means.1.refs_0_, f32[24,128]{1,0:T(8,128)S(1)} %collective-permute-done.8.refs_1_, f32[24,128]{1,0:T(8,128)S(1)} %collective-permute-done.9.refs_2_, f32[24,128]{1,0:T(8,128)S(1)} %collective-permute-done.10.refs_3_), custom_call_target="tpu_custom_call" | custom-call | tf_op jit(solution)/shard_map/total/pallas_call | solution.py:577
  (11 shorter events, 0.0 us)
Async XLA Ops:
  1.9 5.2 %collective-permute-start = (bf16[224,128]{1,0:T(8,128)(2,1)S(1)}, bf16[224,128]{1,0:T(8,128)(2,1)S(1)}, u32[]{:S(2)}, u32[]{:S(2)}) collective-permute-start(bf16[224,128]{1,0:T(8,128)(2,1)S(1)} %get-tuple-element.11), channel_id=1, source_target_pairs={{0,8},{4,12},{8,0},{12,4},{16,24},{20,28},{24,16},{28,20},{1,9},{5... | collective-permute-start | bytes 172040 | tf_op jit(solution)/shard_map/ppermute | solution.py:474
  4.9 4.2 %collective-permute-start.1 = (bf16[224,128]{1,0:T(8,128)(2,1)S(1)}, bf16[224,128]{1,0:T(8,128)(2,1)S(1)}, u32[]{:S(2)}, u32[]{:S(2)}) collective-permute-start(bf16[224,128]{1,0:T(8,128)(2,1)S(1)} %get-tuple-element.12), channel_id=1, source_target_pairs={{0,16},{4,20},{8,24},{12,28},{16,0},{20,4},{24,8},{28,12},{1,17},{... | collective-permute-start | bytes 172040 | tf_op jit(solution)/shard_map/ppermute | solution.py:474
  6.4 5.1 %collective-permute-start.2 = (bf16[224,128]{1,0:T(8,128)(2,1)S(1)}, bf16[224,128]{1,0:T(8,128)(2,1)S(1)}, u32[]{:S(2)}, u32[]{:S(2)}) collective-permute-start(bf16[224,128]{1,0:T(8,128)(2,1)S(1)} %get-tuple-element.13), channel_id=1, source_target_pairs={{0,24},{4,28},{8,16},{12,20},{16,8},{20,12},{24,0},{28,4},{1,25},{... | collective-permute-start | bytes 172040 | tf_op jit(solution)/shard_map/ppermute | solution.py:474
  11.5 1.4 %copy-start.1 = (f32[2,6]{1,0:T(2,128)S(1)}, f32[2,6]{1,0:T(2,128)}, u32[]{:S(2)}) copy-start(f32[2,6]{1,0:T(2,128)} %refs_5_.1) | copy-start | bytes 148
  11.5 1.4 %copy-start.2 = (f32[2,6]{1,0:T(2,128)S(1)}, f32[2,6]{1,0:T(2,128)}, u32[]{:S(2)}) copy-start(f32[2,6]{1,0:T(2,128)} %refs_6_.1) | copy-start | bytes 148
  11.5 1.4 %collective-permute-start.3 = (bf16[512,128]{1,0:T(8,128)(2,1)S(1)}, bf16[512,128]{1,0:T(8,128)(2,1)S(1)}, u32[]{:S(2)}, u32[]{:S(2)}) collective-permute-start(bf16[512,128]{1,0:T(8,128)(2,1)S(1)} %pass.2), channel_id=1, source_target_pairs={{0,4},{4,0},{8,12},{12,8},{16,20},{20,16},{24,28},{28,24},{1,5},{5... | collective-permute-start | bytes 393224 | tf_op jit(solution)/shard_map/ppermute | solution.py:483
  21.1 3.9 %collective-permute-start.4 = (f32[48,128]{1,0:T(8,128)S(1)}, f32[48,128]{1,0:T(8,128)S(1)}, u32[]{:S(2)}, u32[]{:S(2)}) collective-permute-start(f32[48,128]{1,0:T(8,128)S(1)} %get-tuple-element.15), channel_id=1, source_target_pairs={{0,8},{4,12},{8,0},{12,4},{16,24},{20,28},{24,16},{28,20},{1,9},{5... | collective-permute-start | bytes 73736 | tf_op jit(solution)/shard_map/ppermute | solution.py:474
  21.7 3.9 %collective-permute-start.5 = (f32[48,128]{1,0:T(8,128)S(1)}, f32[48,128]{1,0:T(8,128)S(1)}, u32[]{:S(2)}, u32[]{:S(2)}) collective-permute-start(f32[48,128]{1,0:T(8,128)S(1)} %get-tuple-element.16), channel_id=1, source_target_pairs={{0,16},{4,20},{8,24},{12,28},{16,0},{20,4},{24,8},{28,12},{1,17},{... | collective-permute-start | bytes 73736 | tf_op jit(solution)/shard_map/ppermute | solution.py:474
  21.8 4.7 %collective-permute-start.6 = (f32[48,128]{1,0:T(8,128)S(1)}, f32[48,128]{1,0:T(8,128)S(1)}, u32[]{:S(2)}, u32[]{:S(2)}) collective-permute-start(f32[48,128]{1,0:T(8,128)S(1)} %get-tuple-element.17), channel_id=1, source_target_pairs={{0,24},{4,28},{8,16},{12,20},{16,8},{20,12},{24,0},{28,4},{1,25},{... | collective-permute-start | bytes 73736 | tf_op jit(solution)/shard_map/ppermute | solution.py:474
  26.5 1.2 %copy-start = (s32[64,6]{0,1:T(8,128)S(1)}, s32[64,6]{0,1:T(8,128)}, u32[]{:S(2)}) copy-start(s32[64,6]{0,1:T(8,128)} %param.21) | copy-start | bytes 4612
  26.5 1.2 %collective-permute-start.7 = (f32[96,128]{1,0:T(8,128)S(1)}, f32[96,128]{1,0:T(8,128)S(1)}, u32[]{:S(2)}, u32[]{:S(2)}) collective-permute-start(f32[96,128]{1,0:T(8,128)S(1)} %pass.3), channel_id=1, source_target_pairs={{0,4},{4,0},{8,12},{12,8},{16,20},{20,16},{24,28},{28,24},{1,5},{5... | collective-permute-start | bytes 147464 | tf_op jit(solution)/shard_map/ppermute | solution.py:483
  27.9 5.7 %collective-permute-start.10 = (f32[24,128]{1,0:T(8,128)S(1)}, f32[24,128]{1,0:T(8,128)S(1)}, u32[]{:S(2)}, u32[]{:S(2)}) collective-permute-start(f32[24,128]{1,0:T(8,128)S(1)} %means.1.refs_0_), channel_id=1, source_target_pairs={{0,3},{1,2},{2,1},{3,0},{4,7},{5,6},{6,5},{7,4},{8,11},{9,10},{10,... | collective-permute-start | bytes 36872 | tf_op jit(solution)/shard_map/ppermute | solution.py:565
  32.0 4.6 %collective-permute-start.9 = (f32[24,128]{1,0:T(8,128)S(1)}, f32[24,128]{1,0:T(8,128)S(1)}, u32[]{:S(2)}, u32[]{:S(2)}) collective-permute-start(f32[24,128]{1,0:T(8,128)S(1)} %means.1.refs_0_), channel_id=1, source_target_pairs={{0,2},{1,3},{2,0},{3,1},{4,6},{5,7},{6,4},{7,5},{8,10},{9,11},{10,... | collective-permute-start | bytes 36872 | tf_op jit(solution)/shard_map/ppermute | solution.py:565
  32.0 4.6 %collective-permute-start.8 = (f32[24,128]{1,0:T(8,128)S(1)}, f32[24,128]{1,0:T(8,128)S(1)}, u32[]{:S(2)}, u32[]{:S(2)}) collective-permute-start(f32[24,128]{1,0:T(8,128)S(1)} %means.1.refs_0_), channel_id=1, source_target_pairs={{0,1},{1,0},{2,3},{3,2},{4,5},{5,4},{6,7},{7,6},{8,9},{9,8},{10,11... | collective-permute-start | bytes 36872 | tf_op jit(solution)/shard_map/ppermute | solution.py:565

commit v5 on v4

--- a/solution.py
+++ b/solution.py
@@ -81,9 +81,42 @@
     ]
     for copy in copies:
         copy.start()
-    for copy in copies:
+    for copy in copies[1:]:
         copy.wait()
     me = lax.axis_index("loan")
+    info[...] = jnp.zeros_like(info)
+    values = [region[...].astype(F32), init[...].astype(F32), pool[...].astype(F32)]
+    values += pieces(jnp.log(ltv[...]), 2) + pieces(balance[...], 2)
+    for q, value in enumerate(values):
+        info[q * z.loan_rows : (q + 1) * z.loan_rows, :] = value
+    lane = lax.broadcasted_iota(jnp.int32, (1, LANES), 1)
+    mine = lane // z.dev_slots == lax.rem(me, z.sources)
+
+    def spread(lists):
+        table[...] = jnp.zeros_like(table)
+        table[0 : z.blocks, 0 : z.slots] = lists.astype(F32)
+        wide = table[...]
+        row = wide[0:1, :]
+        for b in range(1, z.blocks):
+            row = row + pltpu.roll(wide, b * z.slots, 1)[b : b + 1, :]
+        wide = row
+        for c in range(1, z.sources):
+            wide = wide + pltpu.roll(jnp.broadcast_to(row, (8, LANES)), c * z.dev_slots, 1)[0:1, :]
+        return jnp.where(mine, wide, 0.0)
+
+    listed = spread(pool_lists[...])
+    high = jnp.floor(listed * (1.0 / 64.0))
+    metro = spread(regions[...])
+    owner = jnp.zeros_like(metro)
+    for k in range(1, z.devs):
+        owner = owner + jnp.where(metro >= float(k * z.metros), 1.0, 0.0)
+    rows = [high, listed - 64.0 * high, owner, metro - owner * float(z.metros)]
+    for i, row in enumerate(rows):
+        info[z.list_row + i : z.list_row + i + 1, :] = row
+    packed = info[...].astype(BF16)
+    for c in range(z.chips):
+        outs[c][2 * z.price_rows :, :] = packed
+    copies[0].wait()
     for g in range(z.groups):
         parts = []
         for h in range(z.fold):
@@ -104,38 +137,6 @@
                 ]
                 first = other * z.price_rows + g * z.width
                 outs[c][first : first + z.width, :] = jnp.concatenate(both, axis=0).astype(BF16)
-    info[...] = jnp.zeros_like(info)
-    values = [region[...].astype(F32), init[...].astype(F32), pool[...].astype(F32)]
-    values += pieces(jnp.log(ltv[...]), 2) + pieces(balance[...], 2)
-    for q, value in enumerate(values):
-        info[q * z.loan_rows : (q + 1) * z.loan_rows, :] = value
-    lane = lax.broadcasted_iota(jnp.int32, (1, LANES), 1)
-    mine = lane // z.dev_slots == lax.rem(me, z.sources)
-
-    def spread(lists):
-        table[...] = jnp.zeros_like(table)
-        table[0 : z.blocks, 0 : z.slots] = lists.astype(F32)
-        wide = table[...]
-        row = wide[0:1, :]
-        for b in range(1, z.blocks):
-            row = row + pltpu.roll(wide, b * z.slots, 1)[b : b + 1, :]
-        wide = row
-        for c in range(1, z.sources):
-            wide = wide + pltpu.roll(jnp.broadcast_to(row, (8, LANES)), c * z.dev_slots, 1)[0:1, :]
-        return jnp.where(mine, wide, 0.0)
-
-    listed = spread(pool_lists[...])
-    high = jnp.floor(listed * (1.0 / 64.0))
-    metro = spread(regions[...])
-    owner = jnp.zeros_like(metro)
-    for k in range(1, z.devs):
-        owner = owner + jnp.where(metro >= float(k * z.metros), 1.0, 0.0)
-    rows = [high, listed - 64.0 * high, owner, metro - owner * float(z.metros)]
-    for i, row in enumerate(rows):
-        info[z.list_row + i : z.list_row + i + 1, :] = row
-    packed = info[...].astype(BF16)
-    for c in range(z.chips):
-        outs[c][2 * z.price_rows :, :] = packed
 
 
 def pass_kernel(z, rows, *refs):
@@ -198,7 +199,14 @@
         total = info[group * z.sources, z.list_row : z.list_row + 4, :]
         for i in range(1, z.sources):
             total = total + info[group * z.sources + i, z.list_row : z.list_row + 4, :]
-        lists[group] = total
+        ordered = total
+        for i in range(1, z.sources):
+            swapped = None
+            for c in range(z.sources):
+                part = rolled(total, (c - (c ^ i)) * z.dev_slots)
+                swapped = part if c == 0 else jnp.where(lane // z.dev_slots == c, part, swapped)
+            ordered = jnp.where(lax.rem(me, z.sources) == i, swapped, ordered)
+        lists[group] = ordered
 
     keys = z.devs * z.pad
     path = lax.broadcasted_iota(jnp.int32, (z.width, LANES), 0)
@@ -263,21 +271,20 @@
         both = values[j, first : first + z.per, :]
         return jnp.concatenate([both[r : r + 1, :] for r in range(z.per)], axis=1)
 
-    def one_hot(j, b, q):
-        ours = jnp.where(slot_row == row(j, b, q), 1.0, 0.0)
-        place = lax.rem(me ^ j, z.sources)
-        parts = []
-        for i in range(z.sources):
-            here = jnp.where(place == i, ours, 0.0).astype(BF16)
-            parts += [here if k == b else jnp.zeros_like(here) for k in range(z.blocks)]
+    def one_hot(j, i, b, q):
+        ours = jnp.where(slot_row == row(j, b, q), 1.0, 0.0).astype(BF16)
+        parts = [jnp.zeros_like(ours)] * (z.sources * z.blocks)
+        parts[(i % z.sources) * z.blocks + b] = ours
         return jnp.concatenate(parts, axis=0)
 
-    def fill(j, b, moved):
-        chosen = one_hot(j, b, 0)
+    def fill(first, i, b, moved):
+        j = first + i
+        chosen = one_hot(j, i, b, 0)
         chosen = jnp.concatenate([chosen, chosen], axis=0)
         moved[...] = jnp.dot(both_pieces[j // z.sources], chosen, preferred_element_type=F32)
 
-    def run(j, b, moved):
+    def run(first, i, b, moved):
+        j = first + i
         start = row(j, b, 1)
         begins = [start == float(k) for k in range(z.live)]
         balance_rows = [row(j, b, q) for q in (5, 6)]
@@ -355,7 +362,7 @@
         dated[2 * marks :, :] = money.astype(BF16)
         group = j // z.sources
         sums[group] = sums[group] + lax.dot_general(
-            dated[...], one_hot(j, b, 2), (((1,), (1,)), ((), ())), preferred_element_type=F32
+            dated[...], one_hot(j, i, b, 2), (((1,), (1,)), ((), ())), preferred_element_type=F32
         )
 
     moved = (moved_even, moved_odd)
@@ -363,12 +370,13 @@
     unroll = min(8, z.devs)
 
     def source_step(step, carry):
-        order = [(step * unroll + i, b) for i in range(unroll) for b in range(z.blocks)]
+        first = step * unroll
+        order = [(first, i, b) for i in range(unroll) for b in range(z.blocks)]
         fill(*order[0], moved[0])
-        for i, (j, b) in enumerate(order):
+        for i, block in enumerate(order):
             if i + 1 < len(order):
                 fill(*order[i + 1], moved[(i + 1) % 2])
-            run(j, b, moved[i % 2])
+            run(*block, moved[i % 2])
         return carry
 
     lax.fori_loop(0, z.devs // unroll, source_step, 0)

time: 37.4 us -> 37.4 us (level)
  no operation moved by 1% of the time
where the time goes in v5:
time: 37.4 us; the launch traced here: 37.3 us
  starting transfers between devices  12.9 us (34%)
  waiting for transfers between devices  12.4 us (33%)
  Pallas kernels  11.3 us (30%)
  between operations  0.68 us (2%)
    ppermute x6, starting transfers between devices, exchange(): lax.ppermute(parts[c], 'loan', [(i, i ^ 2 * c) for i in range(z.devs)])  8.13 us
    pallas_call x1, Pallas kernels, shards(): pl.pallas_call(functools.partial(months_kernel, z), out_shape=[jax.ShapeD...  8.08 us
    ppermute x6, waiting for transfers between devices, exchange(): lax.ppermute(parts[c], 'loan', [(i, i ^ 2 * c) for i in range(z.devs)])  6.93 us
    ppermute x3, starting transfers between devices, shards(): lax.ppermute(sums, 'path', [(i, i ^ k) for i in range(z.path_devs)])  4.71 us
    ppermute x3, waiting for transfers between devices, shards(): lax.ppermute(sums, 'path', [(i, i ^ k) for i in range(z.path_devs)])  2.94 us
    ppermute x2, waiting for transfers between devices, exchange(): lax.ppermute(passed, 'loan', [(i, i ^ 1) for i in range(z.devs)])  2.56 us
    pallas_call x1, Pallas kernels, shards(): pl.pallas_call(functools.partial(pack_kernel, z), out_shape=[jax.ShapeDty...  1.29 us
    pallas_call x1, Pallas kernels, shards(): pl.pallas_call(functools.partial(paths_kernel, z), out_shape=jax.ShapeDty...  1.01 us
  transfers between devices with their start and end apart: 11, of which 9 were waited for; matrix products, arithmetic and copies ran while one was open for 0% of the time, Pallas kernels for 3%

profile of v5, /device:TPU:0, one launch (start us, length us, event | category | flops | bytes accessed | tf_op | source)
XLA Modules:
  0.0 37.3 jit_solution(11543300988262418868)
XLA Ops:
  0.6 1.3 %pack.1 = (bf16[224,128]{1,0:T(8,128)(2,1)S(1)}, bf16[224,128]{1,0:T(8,128)(2,1)S(1)}, bf16[224,128]{1,0:T(8,128)(2,1)S(1)}, bf16[224,128]{1,0:T(8,128)(2,1)S(1)}) custom-call(bf16[12,52,128]{2,1,0:T(8,128)(2,1)} %refs_0_.1, s32[2,32]{1,0:T(2,128)} %refs_1_.1, s32[2,32]{1,0:T(2,128)} %refs_2_.1, s32[4,128]{1,0:T(4,128)} %bitcast.8, s32[4,128]{1,0:T(4,128)} %bitcast.9, ...), custom_call_target="tpu_custom_call" | custom-call | tf_op jit(solution)/shard_map/pack/pallas_call | solution.py:522
  1.9 3.0 %collective-permute-start = (bf16[224,128]{1,0:T(8,128)(2,1)S(1)}, bf16[224,128]{1,0:T(8,128)(2,1)S(1)}, u32[]{:S(2)}, u32[]{:S(2)}) collective-permute-start(bf16[224,128]{1,0:T(8,128)(2,1)S(1)} %get-tuple-element.11), channel_id=1, source_target_pairs={{0,8},{4,12},{8,0},{12,4},{16,24},{20,28},{24,16},{28,20},{1,9},{5... | collective-permute-start | bytes 172040 | tf_op jit(solution)/shard_map/ppermute | solution.py:482
  5.0 1.5 %collective-permute-start.1 = (bf16[224,128]{1,0:T(8,128)(2,1)S(1)}, bf16[224,128]{1,0:T(8,128)(2,1)S(1)}, u32[]{:S(2)}, u32[]{:S(2)}) collective-permute-start(bf16[224,128]{1,0:T(8,128)(2,1)S(1)} %get-tuple-element.12), channel_id=1, source_target_pairs={{0,16},{4,20},{8,24},{12,28},{16,0},{20,4},{24,8},{28,12},{1,17},{... | collective-permute-start | bytes 172040 | tf_op jit(solution)/shard_map/ppermute | solution.py:482
  6.5 0.0 collective-permute-start.2
  6.5 0.6 %collective-permute-done.refs_1_ = bf16[224,128]{1,0:T(8,128)(2,1)S(1)} collective-permute-done((bf16[224,128]{1,0:T(8,128)(2,1)S(1)}, bf16[224,128]{1,0:T(8,128)(2,1)S(1)}, u32[]{:S(2)}, u32[]{:S(2)}) %collective-permute-start) | collective-permute-done | bytes 57376 | tf_op jit(solution)/shard_map/ppermute | solution.py:482
  7.1 2.0 %collective-permute-done.1.refs_2_ = bf16[224,128]{1,0:T(8,128)(2,1)S(1)} collective-permute-done((bf16[224,128]{1,0:T(8,128)(2,1)S(1)}, bf16[224,128]{1,0:T(8,128)(2,1)S(1)}, u32[]{:S(2)}, u32[]{:S(2)}) %collective-permute-start.1) | collective-permute-done | bytes 57376 | tf_op jit(solution)/shard_map/ppermute | solution.py:482
  9.1 2.4 %collective-permute-done.2.refs_3_ = bf16[224,128]{1,0:T(8,128)(2,1)S(1)} collective-permute-done((bf16[224,128]{1,0:T(8,128)(2,1)S(1)}, bf16[224,128]{1,0:T(8,128)(2,1)S(1)}, u32[]{:S(2)}, u32[]{:S(2)}) %collective-permute-start.2) | collective-permute-done | bytes 57376 | tf_op jit(solution)/shard_map/ppermute | solution.py:482
  11.6 0.1 collective-permute-start.3
  11.7 1.3 %collective-permute-done.3.refs_4_ = bf16[512,128]{1,0:T(8,128)(2,1)S(1)} collective-permute-done((bf16[512,128]{1,0:T(8,128)(2,1)S(1)}, bf16[512,128]{1,0:T(8,128)(2,1)S(1)}, u32[]{:S(2)}, u32[]{:S(2)}) %collective-permute-start.3) | collective-permute-done | bytes 131104 | tf_op jit(solution)/shard_map/ppermute | solution.py:491
  13.0 8.1 %months.1 = (f32[48,128]{1,0:T(8,128)S(1)}, f32[48,128]{1,0:T(8,128)S(1)}, f32[48,128]{1,0:T(8,128)S(1)}, f32[48,128]{1,0:T(8,128)S(1)}) custom-call(bf16[224,128]{1,0:T(8,128)(2,1)S(1)} %get-tuple-element.10.refs_0_, bf16[224,128]{1,0:T(8,128)(2,1)S(1)} %collective-permute-done.refs_1_, bf16[224,128]{1,0:T(8,128)(2,1)S(1)} %collective-permute-done.1.refs_2_, ...), custom_call_target="tpu_custom_call" | custom-call | tf_op jit(solution)/shard_map/months/pallas_call | solution.py:540
  21.1 0.6 %collective-permute-start.4 = (f32[48,128]{1,0:T(8,128)S(1)}, f32[48,128]{1,0:T(8,128)S(1)}, u32[]{:S(2)}, u32[]{:S(2)}) collective-permute-start(f32[48,128]{1,0:T(8,128)S(1)} %get-tuple-element.15), channel_id=1, source_target_pairs={{0,8},{4,12},{8,0},{12,4},{16,24},{20,28},{24,16},{28,20},{1,9},{5... | collective-permute-start | bytes 73736 | tf_op jit(solution)/shard_map/ppermute | solution.py:482
  21.7 0.1 collective-permute-start.5
  21.8 2.8 %collective-permute-start.6 = (f32[48,128]{1,0:T(8,128)S(1)}, f32[48,128]{1,0:T(8,128)S(1)}, u32[]{:S(2)}, u32[]{:S(2)}) collective-permute-start(f32[48,128]{1,0:T(8,128)S(1)} %get-tuple-element.17), channel_id=1, source_target_pairs={{0,24},{4,28},{8,16},{12,20},{16,8},{20,12},{24,0},{28,4},{1,25},{... | collective-permute-start | bytes 73736 | tf_op jit(solution)/shard_map/ppermute | solution.py:482
  24.6 0.3 collective-permute-done.4.refs_1_
  25.0 0.6 %collective-permute-done.5.refs_2_ = f32[48,128]{1,0:T(8,128)S(1)} collective-permute-done((f32[48,128]{1,0:T(8,128)S(1)}, f32[48,128]{1,0:T(8,128)S(1)}, u32[]{:S(2)}, u32[]{:S(2)}) %collective-permute-start.5) | collective-permute-done | bytes 24608 | tf_op jit(solution)/shard_map/ppermute | solution.py:482
  25.6 0.9 %collective-permute-done.6.refs_3_ = f32[48,128]{1,0:T(8,128)S(1)} collective-permute-done((f32[48,128]{1,0:T(8,128)S(1)}, f32[48,128]{1,0:T(8,128)S(1)}, u32[]{:S(2)}, u32[]{:S(2)}) %collective-permute-start.6) | collective-permute-done | bytes 24608 | tf_op jit(solution)/shard_map/ppermute | solution.py:482
  26.5 1.2 %collective-permute-done.7.refs_4_ = f32[96,128]{1,0:T(8,128)S(1)} collective-permute-done((f32[96,128]{1,0:T(8,128)S(1)}, f32[96,128]{1,0:T(8,128)S(1)}, u32[]{:S(2)}, u32[]{:S(2)}) %collective-permute-start.7) | collective-permute-done | bytes 49184 | tf_op jit(solution)/shard_map/ppermute | solution.py:491
  27.8 0.2 means.1.refs_0_
  27.9 4.1 %collective-permute-start.10 = (f32[24,128]{1,0:T(8,128)S(1)}, f32[24,128]{1,0:T(8,128)S(1)}, u32[]{:S(2)}, u32[]{:S(2)}) collective-permute-start(f32[24,128]{1,0:T(8,128)S(1)} %means.1.refs_0_), channel_id=1, source_target_pairs={{0,3},{1,2},{2,1},{3,0},{4,7},{5,6},{6,5},{7,4},{8,11},{9,10},{10,... | collective-permute-start | bytes 36872 | tf_op jit(solution)/shard_map/ppermute | solution.py:573
  32.0 0.6 %collective-permute-start.8 = (f32[24,128]{1,0:T(8,128)S(1)}, f32[24,128]{1,0:T(8,128)S(1)}, u32[]{:S(2)}, u32[]{:S(2)}) collective-permute-start(f32[24,128]{1,0:T(8,128)S(1)} %means.1.refs_0_), channel_id=1, source_target_pairs={{0,1},{1,0},{2,3},{3,2},{4,5},{5,4},{6,7},{7,6},{8,9},{9,8},{10,11... | collective-permute-start | bytes 36872 | tf_op jit(solution)/shard_map/ppermute | solution.py:573
  32.7 1.0 %paths.1 = f32[6,64,128]{2,1,0:T(8,128)} custom-call(f32[48,128]{1,0:T(8,128)S(1)} %get-tuple-element.14.refs_0_, f32[48,128]{1,0:T(8,128)S(1)} %collective-permute-done.4.refs_1_, f32[48,128]{1,0:T(8,128)S(1)} %collective-permute-done.5.refs_2_, f32[48,128]{1,0:T(8,128)S(1)} %collective-permute-done.6.refs_3_, ...), custom_call_target="tpu_custom_call" | custom-call | tf_op jit(solution)/shard_map/paths/pallas_call | solution.py:576
  33.7 0.0 collective-permute-done.10.refs_3_
  33.7 2.9 %collective-permute-done.9.refs_2_ = f32[24,128]{1,0:T(8,128)S(1)} collective-permute-done((f32[24,128]{1,0:T(8,128)S(1)}, f32[24,128]{1,0:T(8,128)S(1)}, u32[]{:S(2)}, u32[]{:S(2)}) %collective-permute-start.9) | collective-permute-done | bytes 12320 | tf_op jit(solution)/shard_map/ppermute | solution.py:573
  36.6 0.7 %total.1 = f32[6,3,64]{2,1,0:T(4,128)} custom-call(f32[24,128]{1,0:T(8,128)S(1)} %means.1.refs_0_, f32[24,128]{1,0:T(8,128)S(1)} %collective-permute-done.8.refs_1_, f32[24,128]{1,0:T(8,128)S(1)} %collective-permute-done.9.refs_2_, f32[24,128]{1,0:T(8,128)S(1)} %collective-permute-done.10.refs_3_), custom_call_target="tpu_custom_call" | custom-call | tf_op jit(solution)/shard_map/total/pallas_call | solution.py:585
  (11 shorter events, 0.0 us)
Async XLA Ops:
  1.9 5.2 %collective-permute-start = (bf16[224,128]{1,0:T(8,128)(2,1)S(1)}, bf16[224,128]{1,0:T(8,128)(2,1)S(1)}, u32[]{:S(2)}, u32[]{:S(2)}) collective-permute-start(bf16[224,128]{1,0:T(8,128)(2,1)S(1)} %get-tuple-element.11), channel_id=1, source_target_pairs={{0,8},{4,12},{8,0},{12,4},{16,24},{20,28},{24,16},{28,20},{1,9},{5... | collective-permute-start | bytes 172040 | tf_op jit(solution)/shard_map/ppermute | solution.py:482
  5.0 4.2 %collective-permute-start.1 = (bf16[224,128]{1,0:T(8,128)(2,1)S(1)}, bf16[224,128]{1,0:T(8,128)(2,1)S(1)}, u32[]{:S(2)}, u32[]{:S(2)}) collective-permute-start(bf16[224,128]{1,0:T(8,128)(2,1)S(1)} %get-tuple-element.12), channel_id=1, source_target_pairs={{0,16},{4,20},{8,24},{12,28},{16,0},{20,4},{24,8},{28,12},{1,17},{... | collective-permute-start | bytes 172040 | tf_op jit(solution)/shard_map/ppermute | solution.py:482
  6.5 5.1 %collective-permute-start.2 = (bf16[224,128]{1,0:T(8,128)(2,1)S(1)}, bf16[224,128]{1,0:T(8,128)(2,1)S(1)}, u32[]{:S(2)}, u32[]{:S(2)}) collective-permute-start(bf16[224,128]{1,0:T(8,128)(2,1)S(1)} %get-tuple-element.13), channel_id=1, source_target_pairs={{0,24},{4,28},{8,16},{12,20},{16,8},{20,12},{24,0},{28,4},{1,25},{... | collective-permute-start | bytes 172040 | tf_op jit(solution)/shard_map/ppermute | solution.py:482
  11.6 1.4 %copy-start.1 = (f32[2,6]{1,0:T(2,128)S(1)}, f32[2,6]{1,0:T(2,128)}, u32[]{:S(2)}) copy-start(f32[2,6]{1,0:T(2,128)} %refs_5_.1) | copy-start | bytes 148
  11.6 1.4 %copy-start.2 = (f32[2,6]{1,0:T(2,128)S(1)}, f32[2,6]{1,0:T(2,128)}, u32[]{:S(2)}) copy-start(f32[2,6]{1,0:T(2,128)} %refs_6_.1) | copy-start | bytes 148
  11.6 1.4 %collective-permute-start.3 = (bf16[512,128]{1,0:T(8,128)(2,1)S(1)}, bf16[512,128]{1,0:T(8,128)(2,1)S(1)}, u32[]{:S(2)}, u32[]{:S(2)}) collective-permute-start(bf16[512,128]{1,0:T(8,128)(2,1)S(1)} %pass.2), channel_id=1, source_target_pairs={{0,4},{4,0},{8,12},{12,8},{16,20},{20,16},{24,28},{28,24},{1,5},{5... | collective-permute-start | bytes 393224 | tf_op jit(solution)/shard_map/ppermute | solution.py:491
  21.1 3.9 %collective-permute-start.4 = (f32[48,128]{1,0:T(8,128)S(1)}, f32[48,128]{1,0:T(8,128)S(1)}, u32[]{:S(2)}, u32[]{:S(2)}) collective-permute-start(f32[48,128]{1,0:T(8,128)S(1)} %get-tuple-element.15), channel_id=1, source_target_pairs={{0,8},{4,12},{8,0},{12,4},{16,24},{20,28},{24,16},{28,20},{1,9},{5... | collective-permute-start | bytes 73736 | tf_op jit(solution)/shard_map/ppermute | solution.py:482
  21.7 3.9 %collective-permute-start.5 = (f32[48,128]{1,0:T(8,128)S(1)}, f32[48,128]{1,0:T(8,128)S(1)}, u32[]{:S(2)}, u32[]{:S(2)}) collective-permute-start(f32[48,128]{1,0:T(8,128)S(1)} %get-tuple-element.16), channel_id=1, source_target_pairs={{0,16},{4,20},{8,24},{12,28},{16,0},{20,4},{24,8},{28,12},{1,17},{... | collective-permute-start | bytes 73736 | tf_op jit(solution)/shard_map/ppermute | solution.py:482
  21.8 4.7 %collective-permute-start.6 = (f32[48,128]{1,0:T(8,128)S(1)}, f32[48,128]{1,0:T(8,128)S(1)}, u32[]{:S(2)}, u32[]{:S(2)}) collective-permute-start(f32[48,128]{1,0:T(8,128)S(1)} %get-tuple-element.17), channel_id=1, source_target_pairs={{0,24},{4,28},{8,16},{12,20},{16,8},{20,12},{24,0},{28,4},{1,25},{... | collective-permute-start | bytes 73736 | tf_op jit(solution)/shard_map/ppermute | solution.py:482
  26.5 1.2 %copy-start = (s32[64,6]{0,1:T(8,128)S(1)}, s32[64,6]{0,1:T(8,128)}, u32[]{:S(2)}) copy-start(s32[64,6]{0,1:T(8,128)} %param.21) | copy-start | bytes 4612
  26.5 1.2 %collective-permute-start.7 = (f32[96,128]{1,0:T(8,128)S(1)}, f32[96,128]{1,0:T(8,128)S(1)}, u32[]{:S(2)}, u32[]{:S(2)}) collective-permute-start(f32[96,128]{1,0:T(8,128)S(1)} %pass.3), channel_id=1, source_target_pairs={{0,4},{4,0},{8,12},{12,8},{16,20},{20,16},{24,28},{28,24},{1,5},{5... | collective-permute-start | bytes 147464 | tf_op jit(solution)/shard_map/ppermute | solution.py:491
  27.9 5.7 %collective-permute-start.10 = (f32[24,128]{1,0:T(8,128)S(1)}, f32[24,128]{1,0:T(8,128)S(1)}, u32[]{:S(2)}, u32[]{:S(2)}) collective-permute-start(f32[24,128]{1,0:T(8,128)S(1)} %means.1.refs_0_), channel_id=1, source_target_pairs={{0,3},{1,2},{2,1},{3,0},{4,7},{5,6},{6,5},{7,4},{8,11},{9,10},{10,... | collective-permute-start | bytes 36872 | tf_op jit(solution)/shard_map/ppermute | solution.py:573
  32.0 4.6 %collective-permute-start.9 = (f32[24,128]{1,0:T(8,128)S(1)}, f32[24,128]{1,0:T(8,128)S(1)}, u32[]{:S(2)}, u32[]{:S(2)}) collective-permute-start(f32[24,128]{1,0:T(8,128)S(1)} %means.1.refs_0_), channel_id=1, source_target_pairs={{0,2},{1,3},{2,0},{3,1},{4,6},{5,7},{6,4},{7,5},{8,10},{9,11},{10,... | collective-permute-start | bytes 36872 | tf_op jit(solution)/shard_map/ppermute | solution.py:573
  32.0 4.6 %collective-permute-start.8 = (f32[24,128]{1,0:T(8,128)S(1)}, f32[24,128]{1,0:T(8,128)S(1)}, u32[]{:S(2)}, u32[]{:S(2)}) collective-permute-start(f32[24,128]{1,0:T(8,128)S(1)} %means.1.refs_0_), channel_id=1, source_target_pairs={{0,1},{1,0},{2,3},{3,2},{4,5},{5,4},{6,7},{7,6},{8,9},{9,8},{10,11... | collective-permute-start | bytes 36872 | tf_op jit(solution)/shard_map/ppermute | solution.py:573
